TPU v7x, 512 devices: a whole 4x8x8 slice. The times are simulated.
512 devices in a mesh: band: 128 (over y, z, core), lon: 4 (over x).
Axes of the slice: x: 4, y: 8, z: 8, core: 2. Of those that a mesh axis runs over, the one named last changes fastest.
Arguments:
- state: bfloat16 [822, 256, 2048], P(None, 'band', 'lon'), may hold values from -6 to 6
- kernel: float32 [822, 3, 3], replicated, may hold values from -6 to 6
- w_state: bfloat16 [256, 822], replicated, may hold values from -0.21875 to 0.21875
- w_conv: bfloat16 [256, 822], replicated, may hold values from -0.21875 to 0.21875
- w_adj: bfloat16 [256, 822], replicated, may hold values from -0.875 to 0.875
- bias_in: float32 [256], replicated, may hold values from -6 to 6
- w_out: bfloat16 [822, 256], replicated, may hold values from -0.375 to 0.375
- obs_op: bfloat16 [96, 822], replicated, may hold values from -0.078125 to 0.078125
- observations: float32 [96, 128, 512], P(None, 'band', 'lon'), may hold values from -12 to 12
- obs_mask: int32 [96, 128, 512], P(None, 'band', 'lon'), may hold values 0 or 1
- dual_in: bfloat16 [96, 128, 512], P(None, 'band', 'lon'), may hold values from -6 to 6
- dual_res: bfloat16 [256, 96], replicated, may hold values from -0.625 to 0.625
- dual_prev: bfloat16 [256, 96], replicated, may hold values from -0.625 to 0.625
- dual_bias: float32 [256], replicated, may hold values from -6 to 6
- dual_out_w: bfloat16 [96, 256], replicated, may hold values from -0.375 to 0.375
- footprint: int32 [128, 4, 8, 4], P('band', 'lon'), may hold values from 0 to 127, all different within a row; in each aligned block of 8 rows (0 to 7, 8 to 15, ..., all dimensions but the last counted through in order) at most 2 rows name the same one
Outputs:
- state_out: bfloat16 [822, 256, 2048], P(None, 'band', 'lon')
- dual_out: bfloat16 [96, 128, 512], P(None, 'band', 'lon')
Inputs may be any that keep to these rules, and one draw needn't show every extreme that they name: `footprint`: within the 8 column blocks of one pair (b, l), the 4 entries of a block differ, and no value appears more than 2 times; in some pairs one value appears exactly 2 times.
All inputs are finite; a program needn't handle non-finite values. No bound on the sum of `obs_mask` on one device may be relied on, other than what follows from the above.
Results may differ from a plain program's by a relative error of at most 0.0075.
Values may be sent and summed in bfloat16 or wider, within the bound.
No kernel may reach another device: no remote copies, remote signals or barrier semaphores. Data moves between devices by JAX's collectives and lax.ppermute only.
A program may use at most 64 MiB of HBM per device.

v0:
```python
import jax
import jax.numpy as jnp
from jax import lax
from jax.sharding import PartitionSpec as P

PIX = 128
TOP = 4


def extended(value, sides, width, wrap):
    for axis, dim in sides:
        count, length = (lax.axis_size(axis), value.shape[dim])
        up = [(i, (i + 1) % count) for i in range(count if wrap else count - 1)]
        down = [(j, i) for i, j in up]
        last = lax.slice_in_dim(value, length - width, length, axis=dim)
        initial = lax.slice_in_dim(value, 0, width, axis=dim)
        before = lax.ppermute(last, axis, up)
        after = lax.ppermute(initial, axis, down)
        value = jnp.concatenate([before, value, after], axis=dim)
    return value


def on_device(
    state,
    kernel,
    w_state,
    w_conv,
    w_adj,
    bias_in,
    w_out,
    obs_op,
    observations,
    obs_mask,
    dual_in,
    dual_res,
    dual_prev,
    dual_bias,
    dual_out_w,
    footprint,
):
    channels, lat_rows, lon_cols = state.shape
    radiance = obs_op.shape[0]
    owners = lax.axis_size("band")
    nblocks = lat_rows * lon_cols // PIX
    routes = footprint.reshape(nblocks, TOP)
    targets = jnp.arange(owners, dtype=jnp.int32)
    member = (routes[:, :, None] == targets[None, None, :]).astype(jnp.int32)
    cover = jnp.sum(member, axis=1).astype(jnp.bfloat16)
    columns = state.reshape(channels, nblocks, PIX)
    projected = jnp.einsum(
        "rc,ckp->krp", obs_op, columns, preferred_element_type=jnp.float32
    ).astype(jnp.bfloat16)
    partial_sums = jnp.einsum(
        "kd,krp->drp", cover, projected, preferred_element_type=jnp.float32
    ).astype(jnp.bfloat16)
    arrived = lax.all_to_all(partial_sums, "band", split_axis=0, concat_axis=0, tiled=True)
    evolved = jnp.sum(arrived, axis=0, dtype=jnp.float32)
    observed = observations.reshape(radiance, PIX)
    valid = obs_mask.reshape(radiance, PIX)
    dual_now = dual_in.reshape(radiance, PIX)
    departure = jnp.where(valid == 1, evolved - observed, 0.0).astype(jnp.bfloat16)
    pre_dual = jnp.dot(dual_res, departure, preferred_element_type=jnp.float32)
    pre_dual = pre_dual + jnp.dot(dual_prev, dual_now, preferred_element_type=jnp.float32)
    dual_hidden = jax.nn.gelu(pre_dual + dual_bias[:, None]).astype(jnp.bfloat16)
    dual_new = (
        dual_now.astype(jnp.float32)
        + jnp.dot(dual_out_w, dual_hidden, preferred_element_type=jnp.float32)
    ).astype(jnp.bfloat16)
    everyone = lax.all_gather(dual_new[:, None, :], "band", axis=1, tiled=True)
    back_sum = jnp.einsum("kd,rdp->krp", cover, everyone, preferred_element_type=jnp.float32)
    back = back_sum.astype(jnp.bfloat16)
    adjoint = jnp.einsum("rc,krp->ckp", obs_op, back, preferred_element_type=jnp.float32).astype(
        jnp.bfloat16
    )
    adjoint = adjoint.reshape(channels, lat_rows * lon_cols)
    widened = extended(state, (("lon", 2),), 1, True)
    padded = extended(widened, (("band", 1),), 1, False)
    filtered = jnp.zeros((channels, lat_rows, lon_cols), jnp.float32)
    for a in range(3):
        for e in range(3):
            filtered = filtered + kernel[:, a, e][:, None, None] * padded[
                :, a : a + lat_rows, e : e + lon_cols
            ].astype(jnp.float32)
    filtered = filtered.astype(jnp.bfloat16).reshape(channels, lat_rows * lon_cols)
    flat_state = state.reshape(channels, lat_rows * lon_cols)
    pre_state = jnp.dot(w_state, flat_state, preferred_element_type=jnp.float32)
    pre_state = pre_state + jnp.dot(w_conv, filtered, preferred_element_type=jnp.float32)
    pre_state = pre_state + jnp.dot(w_adj, adjoint, preferred_element_type=jnp.float32)
    hidden = jax.nn.gelu(pre_state + bias_in[:, None]).astype(jnp.bfloat16)
    updated = flat_state.astype(jnp.float32) + jnp.dot(
        w_out, hidden, preferred_element_type=jnp.float32
    )
    state_out = updated.astype(jnp.bfloat16).reshape(channels, lat_rows, lon_cols)
    return (state_out, dual_new.reshape(radiance, 1, PIX))


def solution(mesh):
    in_specs = (
        P(None, "band", "lon"),
        P(),
        P(),
        P(),
        P(),
        P(),
        P(),
        P(),
        P(None, "band", "lon"),
        P(None, "band", "lon"),
        P(None, "band", "lon"),
        P(),
        P(),
        P(),
        P(),
        P("band", "lon", None, None),
    )
    out_specs = (P(None, "band", "lon"), P(None, "band", "lon"))
    return jax.shard_map(
        on_device, mesh=mesh, in_specs=in_specs, out_specs=out_specs, check_vma=False
    )
```

profile of v0, /device:TPU:1, one launch (start us, length us, event | category | flops | bytes accessed | tf_op | source)
XLA Modules:
  0.0 219.1 jit_solution(3709809616448602039)
XLA Ops:
  7.2 0.0 copy-start
  7.2 0.0 copy-start.6
  7.2 0.8 convert_reduce_fusion.1
  8.0 4.1 %reshape.35 = bf16[822,8,128]{2,1,0:T(8,128)(2,1)S(1)} reshape(bf16[822,2,512]{2,1,0:T(2,128)(2,1)} %param.16) | data formatting | bytes 3366912 | tf_op jit(solution)/shard_map/reshape | solution.py:49
  12.2 0.0 copy-done.6
  12.2 0.4 fusion.10
  12.6 1.0 convolution_convert_fusion
  13.6 3.7 %copy.65 = bf16[128,96,128]{2,1,0:T(8,128)(2,1)} copy(bf16[128,96,128]{2,0,1:T(8,128)(2,1)S(1)} %convolution_convert_fusion) | data formatting | bytes 6291456 | tf_op jit(solution)/shard_map/convert_element_type | solution.py:55
  17.4 18.9 %all-to-all-start = ((bf16[128,96,128]{2,1,0:T(8,128)(2,1)}), bf16[128,96,128]{2,1,0:T(8,128)(2,1)}, u32[]{:S(2)}, u32[]{:S(2)}) async-start(bf16[128,96,128]{2,1,0:T(8,128)(2,1)} %copy.65), calls=%async_computation | async-start | bytes 6291456 | tf_op jit(solution)/shard_map/all_to_all | solution.py:56
  36.3 0.0 copy-start.11
  36.3 0.0 copy-start.12
  36.4 0.0 copy-start.13
  36.4 0.0 copy-start.14
  36.4 0.0 all-gather.3.cloned.1.call-start
  36.4 0.0 copy-done.7
  36.4 0.1 broadcast_compare_fusion
  36.5 0.0 copy-done.8
  36.5 0.0 copy-done.9
  36.5 0.2 fusion.47
  36.7 72.4 %all-to-all-done = bf16[128,96,128]{2,1,0:T(8,128)(2,1)} async-done(((bf16[128,96,128]{2,1,0:T(8,128)(2,1)}), bf16[128,96,128]{2,1,0:T(8,128)(2,1)}, u32[]{:S(2)}, u32[]{:S(2)}) %all-to-all-start) | async-done | bytes 3145760 | tf_op jit(solution)/shard_map/all_to_all | solution.py:56
  109.2 2.4 %convert_reduce_fusion = f32[96,128]{1,0:T(8,128)S(1)} fusion(bf16[128,96,128]{2,1,0:T(8,128)(2,1)} %all-to-all-done), kind=kLoop, calls=%fused_computation | loop fusion | flops 3133440 | bytes 3194880 | tf_op jit(solution)/shard_map/reduce_sum | solution.py:57
  111.6 0.0 copy-done.11
  111.6 0.0 copy-done.12
  111.6 0.0 copy-done.13
  111.6 0.0 copy-done.14
  111.6 1.0 fusion.16
  112.6 0.0 all-gather.3.cloned.1.call-update
  112.6 4.6 %copy.56 = bf16[822,2,512]{0,2,1:T(8,128)(2,1)S(1)} copy(bf16[822,2,512]{2,1,0:T(2,128)(2,1)} %param.16) | data formatting | bytes 3366912 | tf_op args[0]
  117.3 3.1 %collective-permute-start = (bf16[822,2,1]{0,2,1:T(2,128)(2,1)S(1)}, bf16[822,2,1]{0,2,1:T(2,128)(2,1)S(1)}, u32[]{:S(2)}, u32[]{:S(2)}) collective-permute-start(bf16[822,2,1]{0,2,1:T(2,128)(2,1)S(1)} %get-tuple-element.15), channel_id=1, source_target_pairs={{0,1},{1,2},{2,3},{3,0},{4,5},{5,6},{6,7},{7,4},{8,9},{9,10},{10,1... | collective-permute-start | bytes 9872 | tf_op jit(solution)/shard_map/ppermute | solution.py:17
  120.4 0.0 copy-start.1
  120.4 3.5 %collective-permute-start.1 = (bf16[822,2,1]{0,2,1:T(2,128)(2,1)S(1)}, bf16[822,2,1]{0,2,1:T(2,128)(2,1)S(1)}, u32[]{:S(2)}, u32[]{:S(2)}) collective-permute-start(bf16[822,2,1]{0,2,1:T(2,128)(2,1)S(1)} %get-tuple-element.16), channel_id=1, source_target_pairs={{1,0},{2,1},{3,2},{0,3},{5,4},{6,5},{7,6},{4,7},{9,8},{10,9},{11,1... | collective-permute-start | bytes 9872 | tf_op jit(solution)/shard_map/ppermute | solution.py:18
  123.9 0.0 collective-permute-done
  123.9 1.0 collective-permute-done.1
  124.9 0.5 pad_maximum_fusion.1
  125.4 0.2 fusion.65
  125.6 6.4 %collective-permute-start.2 = (bf16[822,1,514]{0,2,1:T(8,128)(2,1)S(1)}, bf16[822,1,514]{0,2,1:T(8,128)(2,1)S(1)}, u32[]{:S(2)}, u32[]{:S(2)}) collective-permute-start(bf16[822,1,514]{0,2,1:T(8,128)(2,1)S(1)} %get-tuple-element.11), channel_id=1, source_target_pairs={{0,4},{4,8},{8,12},{12,16},{16,20},{20,24},{24,28},{28,32},{32,36}... | collective-permute-start | bytes 2535056 | tf_op jit(solution)/shard_map/ppermute | solution.py:17
  132.0 0.0 copy-start.10
  132.0 0.0 copy-start.4
  132.0 2.2 %collective-permute-start.3 = (bf16[822,1,514]{0,2,1:T(8,128)(2,1)S(1)}, bf16[822,1,514]{0,2,1:T(8,128)(2,1)S(1)}, u32[]{:S(2)}, u32[]{:S(2)}) collective-permute-start(bf16[822,1,514]{0,2,1:T(8,128)(2,1)S(1)} %get-tuple-element.12), channel_id=1, source_target_pairs={{4,0},{8,4},{12,8},{16,12},{20,16},{24,20},{28,24},{32,28},{36,32}... | collective-permute-start | bytes 2535056 | tf_op jit(solution)/shard_map/ppermute | solution.py:18
  134.3 0.0 copy-done.1
  134.3 1.3 pad.19
  135.6 0.4 copy.74
  136.0 0.0 copy-done.10
  136.0 0.0 copy-start.2
  136.0 0.1 slice_reduce_fusion.8
  136.1 0.0 copy-done.4
  136.1 0.8 fusion.67
  136.9 5.9 %collective-permute-done.2 = bf16[822,1,514]{0,2,1:T(8,128)(2,1)S(1)} collective-permute-done((bf16[822,1,514]{0,2,1:T(8,128)(2,1)S(1)}, bf16[822,1,514]{0,2,1:T(8,128)(2,1)S(1)}, u32[]{:S(2)}, u32[]{:S(2)}) %collective-permute-start.2) | collective-permute-done | bytes 845048 | tf_op jit(solution)/shard_map/ppermute | solution.py:17
  142.8 5.0 %collective-permute-done.3 = bf16[822,1,514]{0,2,1:T(8,128)(2,1)S(1)} collective-permute-done((bf16[822,1,514]{0,2,1:T(8,128)(2,1)S(1)}, bf16[822,1,514]{0,2,1:T(8,128)(2,1)S(1)}, u32[]{:S(2)}, u32[]{:S(2)}) %collective-permute-start.3) | collective-permute-done | bytes 845048 | tf_op jit(solution)/shard_map/ppermute | solution.py:18
  147.8 3.5 %maximum_maximum_fusion = (bf16[822,3,514]{0,2,1:T(8,128)(2,1)S(1)}, bf16[822,3,514]{0,2,1:T(8,128)(2,1)S(1)}) fusion(bf16[822,2,1]{0,2,1:T(2,128)(2,1)S(1)} %collective-permute-done.1, bf16[822,2,512]{0,2,1:T(8,128)(2,1)S(1)} %copy.56, bf16[822,2,1]{0,2,1:T(2,128)(2,1)S(1)} %collective-permute-done, bf16[822,1,514]{0,2,1:T(8,128)(2,1)S(1)} %collective-permute-done.2, ...), kind=kLoop, calls=%fused_computation.4 | loop fusion | flops 20280384 | bytes 8450160 | tf_op jit(solution)/shard_map/concatenate | solution.py:19
  151.4 0.0 copy-start.5
  151.4 5.2 %add_convert_fusion = bf16[822,2,512]{0,2,1:T(8,128)(2,1)S(1)} fusion(bf16[822,2,512]{0,2,1:T(8,128)(2,1)S(1)} %copy.56, bf16[822,3,514]{0,2,1:T(8,128)(2,1)S(1)} %get-tuple-element.14, bf16[822,2,1]{0,2,1:T(2,128)(2,1)S(1)} %collective-permute-done.1, bf16[822,2,1]{0,2,1:T(2,128)(2,1)S(1)} %collective-permute-done, ...), kind=kLoop, calls=%fused_computation.1 | loop fusion | flops 27777024 | bytes 13503816 | tf_op jit(solution)/shard_map/convert_element_type | solution.py:84
  156.5 0.8 fusion.6
  157.3 39.5 %all-gather.3.cloned.1.call-done = bf16[96,16384]{1,0:T(8,128)(2,1)} async-done(((bf16[96,128]{1,0:T(8,128)(2,1)}), bf16[96,16384]{1,0:T(8,128)(2,1)}) %all-gather.3.cloned.1.call-update) | async-done | bytes 3145744 | tf_op jit(solution)/shard_map/all_gather | solution.py:69
  196.8 2.8 %copy.75 = bf16[12,8,128,128]{3,2,1,0:T(8,128)(2,1)S(1)} copy(bf16[12,8,128,128]{3,1,2,0:T(8,128)(2,1)} %bitcast.89) | data formatting | bytes 6291456
  199.6 0.5 convolution_convert_fusion.2
  200.1 0.7 fusion.3
  200.8 0.2 copy.68
  201.0 0.0 copy-start.15
  201.1 0.1 pad.20
  201.2 1.7 copy.76
  202.9 0.0 copy-done.3
  202.9 4.2 %fusion = bf16[822,1024]{1,0:T(8,128)(2,1)} fusion(bf16[822,1024]{1,0:T(8,128)(2,1)S(1)} %bitcast.86, bf16[822,256]{1,0:T(8,128)(2,1)S(1)} %copy-done, f32[256,1024]{1,0:T(8,128)S(1)} %fusion.6, bf16[822,1024]{1,0:T(8,128)(2,1)} %bitcast.90, bf16[256,822]{0,1:T(8,128)(2,1)} %param.20, f32[256]{0:T(256)S(1)} %copy-done.15), kind=kOutput, calls=%fused_computation.3 | convolution fusion | flops 867338240 | bytes 6941696 | tf_op jit(solution)/shard_map/dot_general | solution.py:90
  207.1 5.1 %reshape.38 = bf16[822,2,512]{2,1,0:T(2,128)(2,1)} reshape(bf16[822,1024]{1,0:T(8,128)(2,1)} %fusion) | data formatting | bytes 3366912 | tf_op jit(solution)/shard_map/reshape | solution.py:93
  (9 shorter events, 0.0 us)
Async XLA Ops:
  7.2 195.7 %copy-start = (bf16[822,256]{1,0:T(8,128)(2,1)S(1)}, bf16[822,256]{1,0:T(8,128)(2,1)}, u32[]{:S(2)}) copy-start(bf16[822,256]{1,0:T(8,128)(2,1)} %param.22) | copy-start | bytes 1262596
  7.2 5.0 %copy-start.6 = (bf16[96,822]{1,0:T(8,128)(2,1)S(1)}, bf16[96,822]{1,0:T(8,128)(2,1)}, u32[]{:S(2)}) copy-start(bf16[96,822]{1,0:T(8,128)(2,1)} %param.23) | copy-start | bytes 473476
  17.4 19.1 %copy-start.7 = (s32[96,1,128]{2,1,0:T(1,128)S(1)}, s32[96,1,128]{2,1,0:T(1,128)}, u32[]{:S(2)}) copy-start(s32[96,1,128]{2,1,0:T(1,128)} %param.25) | copy-start | bytes 147460
  17.4 19.1 %copy-start.8 = (bf16[256,96]{0,1:T(8,128)(2,1)S(1)}, bf16[256,96]{0,1:T(8,128)(2,1)}, u32[]{:S(2)}) copy-start(bf16[256,96]{0,1:T(8,128)(2,1)} %param.28) | copy-start | bytes 147460
  17.4 19.1 %copy-start.9 = (bf16[96,1,128]{2,0,1:T(8,128)(2,1)S(1)}, bf16[96,1,128]{2,0,1:T(8,128)(2,1)}, u32[]{:S(2)}) copy-start(bf16[96,1,128]{2,0,1:T(8,128)(2,1)} %param.26) | copy-start | bytes 73732
  17.4 91.8 %all-to-all-start = ((bf16[128,96,128]{2,1,0:T(8,128)(2,1)}), bf16[128,96,128]{2,1,0:T(8,128)(2,1)}, u32[]{:S(2)}, u32[]{:S(2)}) async-start(bf16[128,96,128]{2,1,0:T(8,128)(2,1)} %copy.65), calls=%async_computation | async-start | bytes 6291456 | tf_op jit(solution)/shard_map/all_to_all | solution.py:56
  36.3 75.2 %copy-start.11 = (bf16[96,256]{1,0:T(8,128)(2,1)S(1)}, bf16[96,256]{1,0:T(8,128)(2,1)}, u32[]{:S(2)}) copy-start(bf16[96,256]{1,0:T(8,128)(2,1)} %param.30) | copy-start | bytes 147460
  36.3 75.2 %copy-start.12 = (bf16[256,96]{0,1:T(8,128)(2,1)S(1)}, bf16[256,96]{0,1:T(8,128)(2,1)}, u32[]{:S(2)}) copy-start(bf16[256,96]{0,1:T(8,128)(2,1)} %param.27) | copy-start | bytes 147460
  36.4 75.2 %copy-start.13 = (f32[96,1,128]{2,1,0:T(1,128)S(1)}, f32[96,1,128]{2,1,0:T(1,128)}, u32[]{:S(2)}) copy-start(f32[96,1,128]{2,1,0:T(1,128)} %param.24) | copy-start | bytes 147460
  36.4 75.2 %copy-start.14 = (f32[256]{0:T(256)S(1)}, f32[256]{0:T(256)}, u32[]{:S(2)}) copy-start(f32[256]{0:T(256)} %param.29) | copy-start | bytes 3076
  36.4 160.5 %all-gather.3.cloned.1.call-start = ((), (), s32[]{:S(2)}) async-start(), calls=%async_computation.1 | async-start | bytes 3170304 | tf_op jit(solution)/shard_map/all_gather | solution.py:69
  117.3 6.7 %collective-permute-start = (bf16[822,2,1]{0,2,1:T(2,128)(2,1)S(1)}, bf16[822,2,1]{0,2,1:T(2,128)(2,1)S(1)}, u32[]{:S(2)}, u32[]{:S(2)}) collective-permute-start(bf16[822,2,1]{0,2,1:T(2,128)(2,1)S(1)} %get-tuple-element.15), channel_id=1, source_target_pairs={{0,1},{1,2},{2,3},{3,0},{4,5},{5,6},{6,7},{7,4},{8,9},{9,10},{10,1... | collective-permute-start | bytes 9872 | tf_op jit(solution)/shard_map/ppermute | solution.py:17
  120.4 13.9 %copy-start.1 = (bf16[822,2,512]{2,1,0:T(2,128)(2,1)S(1)}, bf16[822,2,512]{2,1,0:T(2,128)(2,1)}, u32[]{:S(2)}) copy-start(bf16[822,2,512]{2,1,0:T(2,128)(2,1)} %param.16) | copy-start | bytes 5050372
  120.4 4.5 %collective-permute-start.1 = (bf16[822,2,1]{0,2,1:T(2,128)(2,1)S(1)}, bf16[822,2,1]{0,2,1:T(2,128)(2,1)S(1)}, u32[]{:S(2)}, u32[]{:S(2)}) collective-permute-start(bf16[822,2,1]{0,2,1:T(2,128)(2,1)S(1)} %get-tuple-element.16), channel_id=1, source_target_pairs={{1,0},{2,1},{3,2},{0,3},{5,4},{6,5},{7,6},{4,7},{9,8},{10,9},{11,1... | collective-permute-start | bytes 9872 | tf_op jit(solution)/shard_map/ppermute | solution.py:18
  125.6 17.2 %collective-permute-start.2 = (bf16[822,1,514]{0,2,1:T(8,128)(2,1)S(1)}, bf16[822,1,514]{0,2,1:T(8,128)(2,1)S(1)}, u32[]{:S(2)}, u32[]{:S(2)}) collective-permute-start(bf16[822,1,514]{0,2,1:T(8,128)(2,1)S(1)} %get-tuple-element.11), channel_id=1, source_target_pairs={{0,4},{4,8},{8,12},{12,16},{16,20},{20,24},{24,28},{28,32},{32,36}... | collective-permute-start | bytes 2535056 | tf_op jit(solution)/shard_map/ppermute | solution.py:17
  132.0 4.0 %copy-start.10 = (f32[822,3,3]{0,2,1:T(4,128)S(1)}, f32[822,3,3]{0,2,1:T(4,128)}, u32[]{:S(2)}) copy-start(f32[822,3,3]{0,2,1:T(4,128)} %param.17) | copy-start | bytes 88780
  132.0 4.1 %copy-start.4 = (bf16[256,822]{0,1:T(8,128)(2,1)S(1)}, bf16[256,822]{0,1:T(8,128)(2,1)}, u32[]{:S(2)}) copy-start(bf16[256,822]{0,1:T(8,128)(2,1)} %param.18) | copy-start | bytes 1262596
  132.0 15.8 %collective-permute-start.3 = (bf16[822,1,514]{0,2,1:T(8,128)(2,1)S(1)}, bf16[822,1,514]{0,2,1:T(8,128)(2,1)S(1)}, u32[]{:S(2)}, u32[]{:S(2)}) collective-permute-start(bf16[822,1,514]{0,2,1:T(8,128)(2,1)S(1)} %get-tuple-element.12), channel_id=1, source_target_pairs={{4,0},{8,4},{12,8},{16,12},{20,16},{24,20},{28,24},{32,28},{36,32}... | collective-permute-start | bytes 2535056 | tf_op jit(solution)/shard_map/ppermute | solution.py:18
  136.0 6.8 %copy-start.2 = (bf16[103,8,2,512]{3,1,2,0:T(8,128)(2,1)}, bf16[103,8,2,512]{3,1,2,0:T(8,128)(2,1)S(1)}, u32[]{:S(2)}) copy-start(bf16[103,8,2,512]{3,1,2,0:T(8,128)(2,1)S(1)} %copy.74) | copy-start | bytes 5062660
  151.4 5.2 %copy-start.5 = (bf16[256,822]{0,1:T(8,128)(2,1)S(1)}, bf16[256,822]{0,1:T(8,128)(2,1)}, u32[]{:S(2)}) copy-start(bf16[256,822]{0,1:T(8,128)(2,1)} %param.19) | copy-start | bytes 1262596
  201.0 1.8 copy-start.3
  201.0 1.8 copy-start.15
Sparse Core Ops, SparseCore 0:
  112.7 84.0 all-gather.2
where the time goes:
time: 220 us; the launch traced here: 219 us
  waiting for transfers between devices  124 us (56%)
  starting transfers between devices  34.2 us (16%)
  local copies, waits for them, and re-layouts  24.5 us (11%)
  between operations  14.4 us (7%)
  other arithmetic  12.5 us (6%)
  matrix products  9.58 us (4%)
    all_to_all x1, waiting for transfers between devices, on_device(): lax.all_to_all(partial_sums, 'band', split_axis=0, concat_axis=0, tiled=T...  72.4 us
    all_gather x1, waiting for transfers between devices, on_device(): everyone = lax.all_gather(dual_new[:, None, :], 'band', axis=1, tiled=True)  39.5 us
    all_to_all x1, starting transfers between devices, on_device(): lax.all_to_all(partial_sums, 'band', split_axis=0, concat_axis=0, tiled=T...  18.9 us
    unnamed x38, local copies, waits for them, and re-layouts  11 us
    ppermute x2, starting transfers between devices, extended(): before = lax.ppermute(last, axis, up)  9.53 us
    ppermute x2, waiting for transfers between devices, extended(): after = lax.ppermute(initial, axis, down)  6.01 us
    ppermute x2, waiting for transfers between devices, extended(): before = lax.ppermute(last, axis, up)  5.89 us
    ppermute x2, starting transfers between devices, extended(): after = lax.ppermute(initial, axis, down)  5.73 us
  transfers between devices with their start and end apart: 6, of which 5 were waited for; matrix products, arithmetic and copies ran while one was open for 8% of the time, Pallas kernels for 0%

commit v1 on v0

v1 whole, which is shorter than its diff:
```python
import math

import jax
import jax.numpy as jnp
from jax import lax
from jax.experimental import pallas as pl
from jax.experimental.pallas import tpu as pltpu
from jax.sharding import PartitionSpec as P

PIX = 128
TOP = 4
SUB = 16

VMEM = pl.BlockSpec(memory_space=pltpu.MemorySpace.VMEM)
SMEM = pl.BlockSpec(memory_space=pltpu.MemorySpace.SMEM)


def across(a, b, dims):
    return lax.dot_general(a, b, (dims, ((), ())), preferred_element_type=jnp.float32)


def project_kernel(op_ref, flat_ref, z_ref):
    z = across(op_ref[...], flat_ref[...], ((1,), (0,))).astype(jnp.bfloat16)
    for k in range(z_ref.shape[0]):
        z_ref[k] = z[:, k * PIX : (k + 1) * PIX]


def scatter_kernel(slot_ref, own_ref, other_ref, out_ref):
    slots, blocks = (out_ref.shape[0], own_ref.shape[0])
    empty = jnp.zeros(out_ref.shape[1:], out_ref.dtype)

    def clear(i, carry):
        out_ref[i] = empty
        return carry

    lax.fori_loop(0, slots, clear, 0, unroll=4)
    for side, ref in enumerate((own_ref, other_ref)):
        for k in range(blocks):
            value = ref[k].astype(jnp.float32)
            for t in range(TOP):
                slot = slot_ref[(side * blocks + k) * TOP + t]

                @pl.when(slot < slots)
                def _(slot=slot, value=value):
                    total = out_ref[slot].astype(jnp.float32) + value
                    out_ref[slot] = total.astype(out_ref.dtype)


def gather_kernel(slot_ref, dual_ref, own_ref, other_ref):
    slots, blocks = (dual_ref.shape[0], own_ref.shape[0])
    for side, ref in enumerate((other_ref, own_ref)):
        side = 1 - side
        for k in range(blocks):
            total = jnp.zeros(dual_ref.shape[1:], jnp.float32)
            for t in range(TOP):
                slot = slot_ref[(side * blocks + k) * TOP + t]
                held = dual_ref[jnp.minimum(slot, slots - 1)].astype(jnp.float32)
                total = total + jnp.where(slot < slots, held, 0.0)
            ref[k] = total.astype(ref.dtype)


def stencil_kernel(
    flat_ref, taps_ref, edge_ref, ws_ref, wc_ref, local_ref, up_ref, down_ref, mixed_ref
):
    channels, columns = flat_ref.shape
    half = columns // 2
    column = lax.broadcasted_iota(jnp.int32, (SUB, half), 1)
    first, last = (column == 0, column == half - 1)

    def step(g, carry):
        rows = pl.ds(pl.multiple_of(g * SUB, SUB), SUB)
        taps = taps_ref[rows, :]
        edge = edge_ref[rows, :].astype(jnp.float32)

        def weight(a, e):
            n = a * 3 + e
            return taps[:, n : n + 1]

        views = []
        for i in range(2):
            x = flat_ref[rows, i * half : (i + 1) * half].astype(jnp.float32)
            left = jnp.where(first, edge[:, i : i + 1], pltpu.roll(x, 1, 1))
            right = jnp.where(last, edge[:, 2 + i : 3 + i], pltpu.roll(x, half - 1, 1))
            views.append((left, x, right))

        def row_sum(a, i):
            left, x, right = views[i]
            return weight(a, 0) * left + weight(a, 1) * x + weight(a, 2) * right

        parts = (
            row_sum(1, 0) + row_sum(2, 1),
            row_sum(0, 0) + row_sum(1, 1),
            row_sum(2, 0),
            row_sum(0, 1),
        )
        for n, part in enumerate(parts):
            mixed_ref[rows, n * half : (n + 1) * half] = part.astype(jnp.bfloat16)
        return carry

    lax.fori_loop(0, channels // SUB, step, 0)
    local_ref[...] = across(ws_ref[...], flat_ref[...], ((0,), (0,))) + across(
        wc_ref[...], mixed_ref[:, :columns], ((0,), (0,))
    )
    sent = across(wc_ref[...], mixed_ref[:, columns:], ((0,), (0,))).astype(jnp.bfloat16)
    up_ref[...] = sent[:, :half]
    down_ref[...] = sent[:, half:]


def update_kernel(
    local_ref, below_ref, above_ref, own_ref, other_ref, lift_ref, bias_ref, wo_ref, flat_ref,
    out_ref, back_ref,
):
    columns = flat_ref.shape[1]
    half = columns // 2
    for k in range(own_ref.shape[0]):
        back = own_ref[k] + other_ref[k].astype(jnp.float32)
        back_ref[:, k * PIX : (k + 1) * PIX] = back.astype(jnp.bfloat16)
    pre = local_ref[...] + across(lift_ref[...], back_ref[...], ((1,), (0,))) + bias_ref[...]
    edges = (above_ref, below_ref)
    for i in range(2):
        part = pre[:, i * half : (i + 1) * half] + edges[i][...].astype(jnp.float32)
        hidden = jax.nn.gelu(part).astype(jnp.bfloat16)
        update = across(wo_ref[...], hidden, ((1,), (0,)))
        before = flat_ref[:, i * half : (i + 1) * half].astype(jnp.float32)
        out_ref[:, i * half : (i + 1) * half] = (before + update).astype(out_ref.dtype)


def like(shape, dtype):
    return jax.ShapeDtypeStruct(shape, dtype)


def on_device(
    state,
    kernel,
    w_state,
    w_conv,
    w_adj,
    bias_in,
    w_out,
    obs_op,
    observations,
    obs_mask,
    dual_in,
    dual_res,
    dual_prev,
    dual_bias,
    dual_out_w,
    footprint,
):
    channels, lat_rows, lon_cols = state.shape
    radiance = obs_op.shape[0]
    hid = w_state.shape[0]
    owners = lax.axis_size("band")
    lon_count = lax.axis_size("lon")
    nblocks = lat_rows * lon_cols // PIX
    columns = lat_rows * lon_cols
    full = -(-channels // SUB) * SUB
    extra = full - channels
    side = math.isqrt(owners // 2)
    slots = side * side
    device = [[[(y * side + z) * 2 + c for c in range(2)] for z in range(side)] for y in range(side)]
    by_y = [[[device[y][z][c] for y in range(side)] for z in range(side)] for c in range(2)]
    by_z = [[[device[y][z][c] for z in range(side)] for y in range(side)] for c in range(2)]
    first, second = (by_y[0] + by_z[1], by_z[0] + by_y[1])
    swap = [(i, i ^ 1) for i in range(owners)]
    core = lax.axis_index("band") % 2

    def exchange(value, groups):
        return lax.all_to_all(
            value, "band", split_axis=0, concat_axis=0, axis_index_groups=groups, tiled=True
        )

    routes = footprint.reshape(nblocks * TOP)
    routes = jnp.concatenate([routes, lax.ppermute(routes, "band", swap)])
    at_y, at_z = (routes // (2 * side), (routes // 2) % side)
    slot = jnp.where(core == 0, at_y * side + at_z, at_z * side + at_y)
    slot = jnp.where(routes % 2 == core, slot, slots)

    flat = jnp.pad(state, ((0, extra), (0, 0), (0, 0))).reshape(full, columns)
    operator = jnp.pad(obs_op, ((0, 0), (0, extra)))
    projected = pl.pallas_call(
        project_kernel,
        out_shape=like((nblocks, radiance, PIX), jnp.bfloat16),
        in_specs=[VMEM, VMEM],
        out_specs=VMEM,
        name="project",
    )(operator, flat)
    projected_other = lax.ppermute(projected, "band", swap)
    shares = pl.pallas_call(
        scatter_kernel,
        out_shape=like((slots, radiance, PIX), jnp.bfloat16),
        in_specs=[SMEM, VMEM, VMEM],
        out_specs=VMEM,
        name="scatter",
    )(slot, projected, projected_other)
    arrived = exchange(shares, first)

    state_late, flat_late, projected_other = lax.optimization_barrier((state, flat, projected_other))
    up = [(i, (i + 1) % lon_count) for i in range(lon_count)]
    down = [(j, i) for i, j in up]
    before = lax.ppermute(state_late[:, :, lon_cols - 1].T, "lon", up)
    after = lax.ppermute(state_late[:, :, 0].T, "lon", down)
    edge = jnp.pad(jnp.concatenate([before, after], axis=0).T, ((0, extra), (0, 4)))
    taps = jnp.pad(kernel.reshape(channels, 9), ((0, extra), (0, 0)))
    local, to_up, to_down = pl.pallas_call(
        stencil_kernel,
        out_shape=(
            like((hid, columns), jnp.float32),
            like((hid, lon_cols), jnp.bfloat16),
            like((hid, lon_cols), jnp.bfloat16),
        ),
        in_specs=[VMEM] * 5,
        out_specs=(VMEM,) * 3,
        scratch_shapes=[pltpu.VMEM((full, 2 * columns), jnp.bfloat16)],
        name="stencil",
    )(
        flat_late,
        taps,
        edge,
        jnp.pad(w_state.T, ((0, extra), (0, 0))),
        jnp.pad(w_conv.T, ((0, extra), (0, 0))),
    )
    onward = [(i, i + 1) for i in range(owners - 1)]
    above = lax.ppermute(to_down, "band", onward)
    below = lax.ppermute(to_up, "band", [(j, i) for i, j in onward])
    lift = across(w_adj, obs_op, ((1,), (1,))).astype(jnp.bfloat16)

    summed = jnp.sum(
        arrived.reshape(side, side, radiance, PIX), axis=0, dtype=jnp.float32
    ).astype(jnp.bfloat16)
    evolved = jnp.sum(exchange(summed, second), axis=0, dtype=jnp.float32)

    observed = observations.reshape(radiance, PIX)
    valid = obs_mask.reshape(radiance, PIX)
    dual_now = dual_in.reshape(radiance, PIX)
    departure = jnp.where(valid == 1, evolved - observed, 0.0).astype(jnp.bfloat16)
    pre_dual = jnp.dot(dual_res, departure, preferred_element_type=jnp.float32)
    pre_dual = pre_dual + jnp.dot(dual_prev, dual_now, preferred_element_type=jnp.float32)
    dual_hidden = jax.nn.gelu(pre_dual + dual_bias[:, None]).astype(jnp.bfloat16)
    dual_new = (
        dual_now.astype(jnp.float32)
        + jnp.dot(dual_out_w, dual_hidden, preferred_element_type=jnp.float32)
    ).astype(jnp.bfloat16)

    column_of = exchange(jnp.broadcast_to(dual_new, (side, radiance, PIX)), second)
    all_of = exchange(
        jnp.broadcast_to(column_of, (side, side, radiance, PIX)).reshape(slots, radiance, PIX), first
    )
    back_own, back_other = pl.pallas_call(
        gather_kernel,
        out_shape=(
            like((nblocks, radiance, PIX), jnp.float32),
            like((nblocks, radiance, PIX), jnp.bfloat16),
        ),
        in_specs=[SMEM, VMEM],
        out_specs=(VMEM, VMEM),
        name="gather",
    )(slot, all_of)
    back_from = lax.ppermute(back_other, "band", swap)
    updated = pl.pallas_call(
        update_kernel,
        out_shape=like((full, columns), jnp.bfloat16),
        in_specs=[VMEM] * 9,
        out_specs=VMEM,
        scratch_shapes=[pltpu.VMEM((radiance, columns), jnp.bfloat16)],
        name="update",
    )(
        local,
        below,
        above,
        back_own,
        back_from,
        lift,
        bias_in[:, None],
        jnp.pad(w_out, ((0, extra), (0, 0))),
        flat,
    )
    state_out = updated.reshape(full, lat_rows, lon_cols)[:channels]
    return (state_out, dual_new.reshape(radiance, 1, PIX))


def solution(mesh):
    in_specs = (
        P(None, "band", "lon"),
        P(),
        P(),
        P(),
        P(),
        P(),
        P(),
        P(),
        P(None, "band", "lon"),
        P(None, "band", "lon"),
        P(None, "band", "lon"),
        P(),
        P(),
        P(),
        P(),
        P("band", "lon", None, None),
    )
    out_specs = (P(None, "band", "lon"), P(None, "band", "lon"))
    return jax.shard_map(
        on_device, mesh=mesh, in_specs=in_specs, out_specs=out_specs, check_vma=False
    )
```

time: 220 us -> 142 us (0.65)
  waiting for transfers between devices: 124 us -> 9.84 us
  blocking collectives: 0 us -> 39.1 us
  Pallas kernels: 0 us -> 24.2 us
  between operations: 14.4 us -> 0.97 us
  other arithmetic: 12.5 us -> 1.65 us
  matrix products: 9.58 us -> 0.8 us
  starting transfers between devices: 34.2 us -> 39.4 us
    all_to_all x1 -> x2, waiting for transfers between devices: 72.4 us -> 8.4 us  [exchange(): lax.all_to_all(value, 'band', split_axis=0, concat_axis=0, axis_index_gro...]
    all_gather x1 -> x0, waiting for transfers between devices: 39.5 us -> none  [on_device(): everyone = lax.all_gather(dual_new[:, None, :], 'band', axis=1, tiled=True)]
    all_to_all x0 -> x2, blocking collectives: none -> 39.1 us  [exchange(): lax.all_to_all(value, 'band', split_axis=0, concat_axis=0, axis_index_gro...]
    pallas_call x0 -> x5, Pallas kernels: none -> 24.2 us  [the longest x1 11.4 us: on_device(): pl.pallas_call(stencil_kernel, out_shape=(like((hid, columns), jnp.float3...]
    ppermute x4 -> x7, starting transfers between devices: 15.3 us -> 28.1 us  [the longest x1 8.73 us: on_device(): projected_other = lax.ppermute(projected, 'band', swap)]
    ppermute x4 -> x7, waiting for transfers between devices: 11.9 us -> 1.44 us  [the longest x1 1.11 us: on_device(): routes = jnp.concatenate([routes, lax.ppermute(routes, 'band', swap)])]
    reshape x2 -> x3, local copies, waits for them, and re-layouts: 9.27 us -> 0.29 us  [the longest x2 0.21 us: on_device(): taps = jnp.pad(kernel.reshape(channels, 9), ((0, extra), (0, 0)))]
    dot_general x7 -> x1, matrix products: 8.38 us -> 0.22 us  [across(): lax.dot_general(a, b, (dims, ((), ())), preferred_element_type=jnp.float32)]
  transfers between devices with their start and end apart: 6 -> 9, of which waited for: 5 -> 3; matrix products, arithmetic and copies ran while one was open for 8% -> 10% of each run, Pallas kernels for 0% -> 10%
where the time goes in v1:
time: 142 us; the launch traced here: 141 us
  starting transfers between devices  39.4 us (28%)
  blocking collectives  39.1 us (28%)
  local copies, waits for them, and re-layouts  25.2 us (18%)
  Pallas kernels  24.2 us (17%)
  waiting for transfers between devices  9.84 us (7%)
  other arithmetic  1.65 us (1%)
    all_to_all x2, blocking collectives, exchange(): lax.all_to_all(value, 'band', split_axis=0, concat_axis=0, axis_index_gro...  39.1 us
    pallas_call x1, Pallas kernels, on_device(): pl.pallas_call(stencil_kernel, out_shape=(like((hid, columns), jnp.float3...  11.4 us
    all_to_all x2, starting transfers between devices, exchange(): lax.all_to_all(value, 'band', split_axis=0, concat_axis=0, axis_index_gro...  11.2 us
    ppermute x1, starting transfers between devices, on_device(): projected_other = lax.ppermute(projected, 'band', swap)  8.73 us
    all_to_all x2, waiting for transfers between devices, exchange(): lax.all_to_all(value, 'band', split_axis=0, concat_axis=0, axis_index_gro...  8.4 us
    optimization_barrier x1, local copies, waits for them, and re-layouts, on_device(): lax.optimization_barrier((state, flat, projected_other))  6.76 us
    ppermute x1, starting transfers between devices, on_device(): below = lax.ppermute(to_up, 'band', [(j, i) for i, j in onward])  6.68 us
    pallas_call x1, Pallas kernels, on_device(): pl.pallas_call(update_kernel, out_shape=like((full, columns), jnp.bfloat1...  4.62 us
  transfers between devices with their start and end apart: 9, of which 3 were waited for; matrix products, arithmetic and copies ran while one was open for 10% of the time, Pallas kernels for 10%

profile of v1, /device:TPU:1, one launch (start us, length us, event | category | flops | bytes accessed | tf_op | source)
XLA Modules:
  0.0 141.1 jit_solution(11602747744108261217)
XLA Ops:
  0.6 0.0 copy-start
  0.6 2.8 %pad.26 = bf16[832,2,512]{2,1,0:T(2,128)(2,1)S(1)} pad(bf16[822,2,512]{2,1,0:T(2,128)(2,1)} %param.16, bf16[]{:T(256)} %constant.62.clone.1), padding=0_10x0_0x0_0 | pad | bytes 3387394 | tf_op jit(solution)/shard_map/jit(_pad)/pad | solution.py:179
  3.4 0.0 copy-start.2
  3.5 1.7 %copy.58 = bf16[104,8,2,512]{3,1,2,0:T(8,128)(2,1)} copy(bf16[104,8,2,512]{3,2,1,0:T(2,128)(2,1)S(1)} %bitcast.57) | data formatting | bytes 3407872
  5.2 0.7 pad.27.op_ref
  5.8 2.7 %project.1.own_ref = bf16[8,96,128]{2,1,0:T(8,128)(2,1)} custom-call(bf16[96,832]{1,0:T(8,128)(2,1)} %pad.27.op_ref, bf16[832,1024]{1,0:T(8,128)(2,1)} %bitcast.54), custom_call_target="tpu_custom_call" | custom-call | tf_op jit(solution)/shard_map/project/pallas_call | solution.py:181
  8.5 8.7 %collective-permute-start = (bf16[8,96,128]{2,1,0:T(8,128)(2,1)}, bf16[8,96,128]{2,1,0:T(8,128)(2,1)S(1)}, u32[]{:S(2)}, u32[]{:S(2)}) collective-permute-start(bf16[8,96,128]{2,1,0:T(8,128)(2,1)} %project.1.own_ref), channel_id=1, source_target_pairs={{0,4},{4,0},{8,12},{12,8},{16,20},{20,16},{24,28},{28,24},{32,36},... | collective-permute-start | bytes 589832 | tf_op jit(solution)/shard_map/ppermute | solution.py:188
  17.3 0.1 copy.52
  17.3 0.1 reshape.36
  17.4 1.9 %collective-permute-start.5 = (s32[32]{0:T(128)S(1)}, s32[32]{0:T(128)S(1)}, u32[]{:S(2)}, u32[]{:S(2)}) collective-permute-start(s32[32]{0:T(128)S(1)} %reshape.36), channel_id=1, source_target_pairs={{0,4},{4,0},{8,12},{12,8},{16,20},{20,16},{24,28},{28,24},{32,36},... | collective-permute-start | bytes 392 | tf_op jit(solution)/shard_map/ppermute | solution.py:174
  19.4 1.1 collective-permute-done.5
  20.5 0.7 compare_select_fusion.2.slot_ref
  21.1 0.0 collective-permute-done.other_ref
  21.2 0.7 copy-done.9
  21.8 3.1 %scatter.1 = bf16[64,96,128]{2,1,0:T(8,128)(2,1)} custom-call(s32[64]{0:T(128)} %compare_select_fusion.2.slot_ref, bf16[8,96,128]{2,1,0:T(8,128)(2,1)} %project.1.own_ref, bf16[8,96,128]{2,1,0:T(8,128)(2,1)} %copy-done.9), custom_call_target="tpu_custom_call" | custom-call | tf_op jit(solution)/shard_map/scatter/pallas_call | solution.py:189
  24.9 28.1 %all_to_all.20 = bf16[64,96,128]{2,1,0:T(8,128)(2,1)S(1)} all-to-all(bf16[64,96,128]{2,1,0:T(8,128)(2,1)} %scatter.1), channel_id=1, replica_groups={{0,64,128,192,256,320,384,448},{8,72,136,200,264,328,392,456},{16,80,14..., dimensions={0} | all-to-all | bytes 3145728 | tf_op jit(solution)/shard_map/all_to_all | solution.py:169
  53.0 0.0 copy-start.18
  53.0 0.0 copy-start.19
  53.0 0.0 copy-start.20
  53.0 0.9 reduce_sum.21
  54.0 6.8 %all-to-all-start.1 = ((bf16[8,96,128]{2,1,0:T(8,128)(2,1)}), bf16[8,96,128]{2,1,0:T(8,128)(2,1)S(1)}, u32[]{:S(2)}, u32[]{:S(2)}) async-start(bf16[8,96,128]{2,1,0:T(8,128)(2,1)} %reduce_sum.21), calls=%async_computation.1 | async-start | bytes 393216 | tf_op jit(solution)/shard_map/all_to_all | solution.py:169
  60.8 0.2 fusion.17
  61.0 8.4 %all-to-all-done.1 = bf16[8,96,128]{2,1,0:T(8,128)(2,1)S(1)} async-done(((bf16[8,96,128]{2,1,0:T(8,128)(2,1)}), bf16[8,96,128]{2,1,0:T(8,128)(2,1)S(1)}, u32[]{:S(2)}, u32[]{:S(2)}) %all-to-all-start.1) | async-done | bytes 196640 | tf_op jit(solution)/shard_map/all_to_all | solution.py:169
  69.4 0.0 copy-done.16
  69.4 0.0 copy-done.17
  69.5 0.4 fusion.3
  69.9 0.0 copy-start.13
  69.9 11.0 %all_to_all.21 = bf16[8,96,128]{2,1,0:T(8,128)(2,1)S(1)} all-to-all(bf16[8,96,128]{2,1,0:T(8,128)(2,1)S(1)} %broadcast_in_dim.20), channel_id=1, replica_groups={{0,8,16,24,32,40,48,56},{64,72,80,88,96,104,112,120},{128,136,144,152,1..., dimensions={0} | all-to-all | bytes 393216 | tf_op jit(solution)/shard_map/all_to_all | solution.py:169
  80.9 1.4 broadcast_in_dim.21
  82.3 4.4 %all-to-all-start.3 = ((bf16[64,96,128]{2,1,0:T(8,128)(2,1)}), bf16[64,96,128]{2,1,0:T(8,128)(2,1)}, u32[]{:S(2)}, u32[]{:S(2)}) async-start(bf16[64,96,128]{2,1,0:T(8,128)(2,1)} %bitcast.58), calls=%async_computation.3 | async-start | bytes 3145728 | tf_op jit(solution)/shard_map/all_to_all | solution.py:169
  86.8 0.0 copy-start.11
  86.8 0.0 copy-start.3
  86.8 0.0 copy-start.4
  86.8 6.8 %copy.49 = bf16[822,2,512]{0,1,2:T(2,128)(2,1)} copy(bf16[822,2,512]{2,1,0:T(2,128)(2,1)S(1)} %copy-done.1) | data formatting | bytes 3366912 | tf_op jit(solution)/shard_map/optimization_barrier | solution.py:198
  93.6 0.7 slice_bitcast_fusion.1
  94.3 3.1 %collective-permute-start.1 = (bf16[2,822]{1,0:T(2,128)(2,1)S(1)}, bf16[2,822]{1,0:T(2,128)(2,1)S(1)}, u32[]{:S(2)}, u32[]{:S(2)}) collective-permute-start(bf16[2,822]{1,0:T(2,128)(2,1)S(1)} %get-tuple-element.16), channel_id=1, source_target_pairs={{0,1},{1,2},{2,3},{3,0},{4,5},{5,6},{6,7},{7,4},{8,9},{9,10},{10,1... | collective-permute-start | bytes 9872 | tf_op jit(solution)/shard_map/ppermute | solution.py:201
  97.4 3.4 %collective-permute-start.2 = (bf16[2,822]{1,0:T(2,128)(2,1)S(1)}, bf16[2,822]{1,0:T(2,128)(2,1)S(1)}, u32[]{:S(2)}, u32[]{:S(2)}) collective-permute-start(bf16[2,822]{1,0:T(2,128)(2,1)S(1)} %get-tuple-element.17), channel_id=1, source_target_pairs={{1,0},{2,1},{3,2},{0,3},{5,4},{6,5},{7,6},{4,7},{9,8},{10,9},{11,1... | collective-permute-start | bytes 9872 | tf_op jit(solution)/shard_map/ppermute | solution.py:202
  100.8 0.2 copy.48
  101.0 0.8 pad.30.ws_ref
  101.8 0.8 pad.31.wc_ref
  102.6 0.8 pad.28.taps_ref
  103.4 0.0 collective-permute-done.1
  103.4 0.0 collective-permute-done.2
  103.5 0.2 copy.51
  103.7 0.7 pad.29.edge_ref
  104.4 11.4 %stencil.1 = (f32[256,1024]{1,0:T(8,128)}, bf16[256,512]{1,0:T(8,128)(2,1)}, bf16[256,512]{1,0:T(8,128)(2,1)}) custom-call(bf16[832,1024]{1,0:T(8,128)(2,1)} %bitcast.55, f32[832,9]{1,0:T(8,128)} %pad.28.taps_ref, bf16[832,8]{1,0:T(8,128)(2,1)} %pad.29.edge_ref, bf16[832,256]{1,0:T(8,128)(2,1)} %pad.30.ws_ref, bf16[832,256]{1,0:T(8,128)(2,1)} %pad.31.wc_ref), custom_call_target="tpu_custom_call" | custom-call | tf_op jit(solution)/shard_map/stencil/pallas_call | solution.py:205
  115.8 6.7 %collective-permute-start.3 = (bf16[256,512]{1,0:T(8,128)(2,1)}, bf16[256,512]{1,0:T(8,128)(2,1)S(1)}, u32[]{:S(2)}, u32[]{:S(2)}) collective-permute-start(bf16[256,512]{1,0:T(8,128)(2,1)} %get-tuple-element.12), channel_id=1, source_target_pairs={{4,0},{8,4},{12,8},{16,12},{20,16},{24,20},{28,24},{32,28},{36,32}... | collective-permute-start | bytes 786440 | tf_op jit(solution)/shard_map/ppermute | solution.py:225
  122.5 2.1 %collective-permute-start.4 = (bf16[256,512]{1,0:T(8,128)(2,1)}, bf16[256,512]{1,0:T(8,128)(2,1)S(1)}, u32[]{:S(2)}, u32[]{:S(2)}) collective-permute-start(bf16[256,512]{1,0:T(8,128)(2,1)} %get-tuple-element.13), channel_id=1, source_target_pairs={{0,4},{4,8},{8,12},{12,16},{16,20},{20,24},{24,28},{28,32},{32,36}... | collective-permute-start | bytes 786440 | tf_op jit(solution)/shard_map/ppermute | solution.py:224
  124.6 0.8 pad.32.wo_ref
  125.4 0.8 copy.56.bias_ref
  126.2 0.0 all-to-all-done.3.dual_ref
  126.2 2.5 %gather.1 = (f32[8,96,128]{2,1,0:T(8,128)}, bf16[8,96,128]{2,1,0:T(8,128)(2,1)}) custom-call(s32[64]{0:T(128)} %compare_select_fusion.2.slot_ref, bf16[64,96,128]{2,1,0:T(8,128)(2,1)} %all-to-all-done.3.dual_ref), custom_call_target="tpu_custom_call" | custom-call | tf_op jit(solution)/shard_map/gather/pallas_call | solution.py:249
  128.7 2.2 %collective-permute-start.6 = (bf16[8,96,128]{2,1,0:T(8,128)(2,1)}, bf16[8,96,128]{2,1,0:T(8,128)(2,1)S(1)}, u32[]{:S(2)}, u32[]{:S(2)}) collective-permute-start(bf16[8,96,128]{2,1,0:T(8,128)(2,1)} %get-tuple-element.15), channel_id=1, source_target_pairs={{0,4},{4,0},{8,12},{12,8},{16,20},{20,16},{24,28},{28,24},{32,36},... | collective-permute-start | bytes 589832 | tf_op jit(solution)/shard_map/ppermute | solution.py:259
  130.9 0.2 convolution_convert_fusion
  131.2 0.7 copy.55.lift_ref
  131.9 0.0 collective-permute-done.3.below_ref
  131.9 0.0 collective-permute-done.4.above_ref
  131.9 0.3 collective-permute-done.6.other_ref
  132.2 0.4 copy-done.6
  132.6 0.1 copy-done.7
  132.7 0.2 copy-done.8
  132.9 4.6 %update.1 = bf16[832,1024]{1,0:T(8,128)(2,1)} custom-call(f32[256,1024]{1,0:T(8,128)} %get-tuple-element.11.local_ref, bf16[256,512]{1,0:T(8,128)(2,1)} %copy-done.6, bf16[256,512]{1,0:T(8,128)(2,1)} %copy-done.7, f32[8,96,128]{2,1,0:T(8,128)} %get-tuple-element.14.own_ref, bf16[8,96,128]{2,1,0:T(8,128)(2,1)} %copy-done.8, bf16[256,96]{1,0:T(8,128)(2,1)} %copy.55.lift_ref, ...), custom_call_target="tpu_custom_call" | custom-call | tf_op jit(solution)/shard_map/update/pallas_call | solution.py:260
  137.5 1.4 %slice-done = bf16[822,1024]{1,0:T(8,128)(2,1)S(1)} async-done(((bf16[832,1024]{1,0:T(8,128)(2,1)}), bf16[822,1024]{1,0:T(8,128)(2,1)S(1)}, s32[]{:S(2)}) %slice-start) | async-done | bytes 1683480 | tf_op jit(solution)/shard_map/slice | solution.py:278
  139.0 2.1 %slice.15 = bf16[822,2,512]{2,1,0:T(2,128)(2,1)} reshape(bf16[822,1024]{1,0:T(8,128)(2,1)S(1)} %slice-done) | data formatting | bytes 3366912 | tf_op jit(solution)/shard_map/slice | solution.py:278
  (32 shorter events, 0.1 us)
Async XLA Ops:
  0.6 130.3 %copy-start = (bf16[256,822]{0,1:T(8,128)(2,1)S(1)}, bf16[256,822]{0,1:T(8,128)(2,1)}, u32[]{:S(2)}) copy-start(bf16[256,822]{0,1:T(8,128)(2,1)} %param.20) | copy-start | bytes 1262596
  3.4 1.7 %copy-start.2 = (bf16[96,822]{1,0:T(8,128)(2,1)S(1)}, bf16[96,822]{1,0:T(8,128)(2,1)}, u32[]{:S(2)}) copy-start(bf16[96,822]{1,0:T(8,128)(2,1)} %param.23) | copy-start | bytes 473476
  5.1 12.1 %copy-start.14 = (s32[1,1,8,4]{2,3,1,0:T(4,128)S(1)}, s32[1,1,8,4]{2,3,1,0:T(4,128)}, u32[]{:S(2)}) copy-start(s32[1,1,8,4]{2,3,1,0:T(4,128)} %param.31) | copy-start | bytes 388
  8.5 12.6 %collective-permute-start = (bf16[8,96,128]{2,1,0:T(8,128)(2,1)}, bf16[8,96,128]{2,1,0:T(8,128)(2,1)S(1)}, u32[]{:S(2)}, u32[]{:S(2)}) collective-permute-start(bf16[8,96,128]{2,1,0:T(8,128)(2,1)} %project.1.own_ref), channel_id=1, source_target_pairs={{0,4},{4,0},{8,12},{12,8},{16,20},{20,16},{24,28},{28,24},{32,36},... | collective-permute-start | bytes 589832 | tf_op jit(solution)/shard_map/ppermute | solution.py:188
  17.4 3.0 %collective-permute-start.5 = (s32[32]{0:T(128)S(1)}, s32[32]{0:T(128)S(1)}, u32[]{:S(2)}, u32[]{:S(2)}) collective-permute-start(s32[32]{0:T(128)S(1)} %reshape.36), channel_id=1, source_target_pairs={{0,4},{4,0},{8,12},{12,8},{16,20},{20,16},{24,28},{28,24},{32,36},... | collective-permute-start | bytes 392 | tf_op jit(solution)/shard_map/ppermute | solution.py:174
  21.1 0.7 copy-start.9
  53.0 7.8 %copy-start.10 = (bf16[256,96]{0,1:T(8,128)(2,1)S(1)}, bf16[256,96]{0,1:T(8,128)(2,1)}, u32[]{:S(2)}) copy-start(bf16[256,96]{0,1:T(8,128)(2,1)} %param.28) | copy-start | bytes 147460
  53.0 7.8 %copy-start.12 = (bf16[96,1,128]{2,0,1:T(8,128)(2,1)S(1)}, bf16[96,1,128]{2,0,1:T(8,128)(2,1)}, u32[]{:S(2)}) copy-start(bf16[96,1,128]{2,0,1:T(8,128)(2,1)} %param.26) | copy-start | bytes 73732
  53.0 16.4 %copy-start.16 = (bf16[96,256]{1,0:T(8,128)(2,1)S(1)}, bf16[96,256]{1,0:T(8,128)(2,1)}, u32[]{:S(2)}) copy-start(bf16[96,256]{1,0:T(8,128)(2,1)} %param.30) | copy-start | bytes 147460
  53.0 16.5 %copy-start.17 = (bf16[256,96]{0,1:T(8,128)(2,1)S(1)}, bf16[256,96]{0,1:T(8,128)(2,1)}, u32[]{:S(2)}) copy-start(bf16[256,96]{0,1:T(8,128)(2,1)} %param.27) | copy-start | bytes 147460
  53.0 16.5 %copy-start.18 = (f32[96,1,128]{2,1,0:T(1,128)S(1)}, f32[96,1,128]{2,1,0:T(1,128)}, u32[]{:S(2)}) copy-start(f32[96,1,128]{2,1,0:T(1,128)} %param.24) | copy-start | bytes 147460
  53.0 16.5 %copy-start.19 = (s32[96,1,128]{2,1,0:T(1,128)S(1)}, s32[96,1,128]{2,1,0:T(1,128)}, u32[]{:S(2)}) copy-start(s32[96,1,128]{2,1,0:T(1,128)} %param.25) | copy-start | bytes 147460
  53.0 16.5 %copy-start.20 = (f32[256]{0:T(256)S(1)}, f32[256]{0:T(256)}, u32[]{:S(2)}) copy-start(f32[256]{0:T(256)} %param.29) | copy-start | bytes 3076
  54.0 15.4 %all-to-all-start.1 = ((bf16[8,96,128]{2,1,0:T(8,128)(2,1)}), bf16[8,96,128]{2,1,0:T(8,128)(2,1)S(1)}, u32[]{:S(2)}, u32[]{:S(2)}) async-start(bf16[8,96,128]{2,1,0:T(8,128)(2,1)} %reduce_sum.21), calls=%async_computation.1 | async-start | bytes 393216 | tf_op jit(solution)/shard_map/all_to_all | solution.py:169
  69.9 12.5 %copy-start.13 = (bf16[96,128]{1,0:T(8,128)(2,1)}, bf16[96,128]{1,0:T(8,128)(2,1)S(1)}, u32[]{:S(2)}) copy-start(bf16[96,128]{1,0:T(8,128)(2,1)S(1)} %fusion.3) | copy-start | bytes 73732
  82.3 4.4 %copy-start.1 = (bf16[822,2,512]{2,1,0:T(2,128)(2,1)S(1)}, bf16[822,2,512]{2,1,0:T(2,128)(2,1)}, u32[]{:S(2)}) copy-start(bf16[822,2,512]{2,1,0:T(2,128)(2,1)} %param.16) | copy-start | bytes 5050372
  82.3 43.9 %all-to-all-start.3 = ((bf16[64,96,128]{2,1,0:T(8,128)(2,1)}), bf16[64,96,128]{2,1,0:T(8,128)(2,1)}, u32[]{:S(2)}, u32[]{:S(2)}) async-start(bf16[64,96,128]{2,1,0:T(8,128)(2,1)} %bitcast.58), calls=%async_computation.3 | async-start | bytes 3145728 | tf_op jit(solution)/shard_map/all_to_all | solution.py:169
  86.8 14.0 %copy-start.11 = (f32[822,3,3]{0,2,1:T(4,128)S(1)}, f32[822,3,3]{0,2,1:T(4,128)}, u32[]{:S(2)}) copy-start(f32[822,3,3]{0,2,1:T(4,128)} %param.17) | copy-start | bytes 88780
  86.8 14.2 %copy-start.3 = (bf16[256,822]{0,1:T(8,128)(2,1)S(1)}, bf16[256,822]{0,1:T(8,128)(2,1)}, u32[]{:S(2)}) copy-start(bf16[256,822]{0,1:T(8,128)(2,1)} %param.18) | copy-start | bytes 1262596
  86.8 15.0 %copy-start.4 = (bf16[256,822]{0,1:T(8,128)(2,1)S(1)}, bf16[256,822]{0,1:T(8,128)(2,1)}, u32[]{:S(2)}) copy-start(bf16[256,822]{0,1:T(8,128)(2,1)} %param.19) | copy-start | bytes 1262596
  94.3 9.2 %collective-permute-start.1 = (bf16[2,822]{1,0:T(2,128)(2,1)S(1)}, bf16[2,822]{1,0:T(2,128)(2,1)S(1)}, u32[]{:S(2)}, u32[]{:S(2)}) collective-permute-start(bf16[2,822]{1,0:T(2,128)(2,1)S(1)} %get-tuple-element.16), channel_id=1, source_target_pairs={{0,1},{1,2},{2,3},{3,0},{4,5},{5,6},{6,7},{7,4},{8,9},{9,10},{10,1... | collective-permute-start | bytes 9872 | tf_op jit(solution)/shard_map/ppermute | solution.py:201
  97.4 6.1 %collective-permute-start.2 = (bf16[2,822]{1,0:T(2,128)(2,1)S(1)}, bf16[2,822]{1,0:T(2,128)(2,1)S(1)}, u32[]{:S(2)}, u32[]{:S(2)}) collective-permute-start(bf16[2,822]{1,0:T(2,128)(2,1)S(1)} %get-tuple-element.17), channel_id=1, source_target_pairs={{1,0},{2,1},{3,2},{0,3},{5,4},{6,5},{7,6},{4,7},{9,8},{10,9},{11,1... | collective-permute-start | bytes 9872 | tf_op jit(solution)/shard_map/ppermute | solution.py:202
  104.4 20.2 %copy-start.5 = (bf16[822,256]{1,0:T(8,128)(2,1)S(1)}, bf16[822,256]{1,0:T(8,128)(2,1)}, u32[]{:S(2)}) copy-start(bf16[822,256]{1,0:T(8,128)(2,1)} %param.22) | copy-start | bytes 1262596
  104.4 21.0 %copy-start.15 = (f32[256]{0:T(256)S(1)}, f32[256]{0:T(256)}, u32[]{:S(2)}) copy-start(f32[256]{0:T(256)} %param.21) | copy-start | bytes 3076
  115.8 16.1 %collective-permute-start.3 = (bf16[256,512]{1,0:T(8,128)(2,1)}, bf16[256,512]{1,0:T(8,128)(2,1)S(1)}, u32[]{:S(2)}, u32[]{:S(2)}) collective-permute-start(bf16[256,512]{1,0:T(8,128)(2,1)} %get-tuple-element.12), channel_id=1, source_target_pairs={{4,0},{8,4},{12,8},{16,12},{20,16},{24,20},{28,24},{32,28},{36,32}... | collective-permute-start | bytes 786440 | tf_op jit(solution)/shard_map/ppermute | solution.py:225
  122.5 9.4 %collective-permute-start.4 = (bf16[256,512]{1,0:T(8,128)(2,1)}, bf16[256,512]{1,0:T(8,128)(2,1)S(1)}, u32[]{:S(2)}, u32[]{:S(2)}) collective-permute-start(bf16[256,512]{1,0:T(8,128)(2,1)} %get-tuple-element.13), channel_id=1, source_target_pairs={{0,4},{4,8},{8,12},{12,16},{16,20},{20,24},{24,28},{28,32},{32,36}... | collective-permute-start | bytes 786440 | tf_op jit(solution)/shard_map/ppermute | solution.py:224
  128.7 3.5 %collective-permute-start.6 = (bf16[8,96,128]{2,1,0:T(8,128)(2,1)}, bf16[8,96,128]{2,1,0:T(8,128)(2,1)S(1)}, u32[]{:S(2)}, u32[]{:S(2)}) collective-permute-start(bf16[8,96,128]{2,1,0:T(8,128)(2,1)} %get-tuple-element.15), channel_id=1, source_target_pairs={{0,4},{4,0},{8,12},{12,8},{16,20},{20,16},{24,28},{28,24},{32,36},... | collective-permute-start | bytes 589832 | tf_op jit(solution)/shard_map/ppermute | solution.py:259
  131.9 0.7 copy-start.6
  131.9 0.8 copy-start.7
  132.2 0.7 copy-start.8
  137.5 1.4 %slice-start = ((bf16[832,1024]{1,0:T(8,128)(2,1)}), bf16[822,1024]{1,0:T(8,128)(2,1)S(1)}, s32[]{:S(2)}) async-start(bf16[832,1024]{1,0:T(8,128)(2,1)} %update.1), calls=%async_computation.4 | async-start | bytes 3375104 | tf_op jit(solution)/shard_map/slice | solution.py:278

commit v2 on v1

v2 whole, which is shorter than its diff:
```python
import math

import jax
import jax.numpy as jnp
from jax import lax
from jax.experimental import pallas as pl
from jax.experimental.pallas import tpu as pltpu
from jax.sharding import PartitionSpec as P

PIX = 128
TOP = 4
SUB = 16
CHUNK = 208

VMEM = pl.BlockSpec(memory_space=pltpu.MemorySpace.VMEM)
SMEM = pl.BlockSpec(memory_space=pltpu.MemorySpace.SMEM)


def across(a, b, dims):
    return lax.dot_general(a, b, (dims, ((), ())), preferred_element_type=jnp.float32)


def edges_kernel(first0_ref, first1_ref, last0_ref, last1_ref, first_ref, last_ref):
    lane = lax.broadcasted_iota(jnp.int32, first_ref.shape, 1)

    def pair(own, other, turn, at):
        turned = pltpu.roll(other[...].astype(jnp.float32), turn, 1)
        return jnp.where(lane == at, own[...].astype(jnp.float32), turned).astype(jnp.bfloat16)

    first_ref[...] = pair(first0_ref, first1_ref, 1, 0)
    last_ref[...] = pair(last0_ref, last1_ref, PIX - 1, PIX - 1)


def scatter_kernel(core_ref, own_route_ref, other_route_ref, own_ref, other_ref, out_ref, slot_ref):
    slots = out_ref.shape[0]
    side = math.isqrt(slots)
    blocks = own_ref.shape[1] // PIX
    core = core_ref[0]
    empty = jnp.zeros(out_ref.shape[1:], out_ref.dtype)

    def clear(i, carry):
        out_ref[i] = empty
        return carry

    lax.fori_loop(0, slots, clear, 0, unroll=8)
    for half, (route_ref, ref) in enumerate(((own_route_ref, own_ref), (other_route_ref, other_ref))):
        for k in range(blocks):
            value = ref[:, k * PIX : (k + 1) * PIX].astype(jnp.float32)
            for t in range(TOP):
                route = route_ref[k * TOP + t]
                at_y, at_z = (route // (2 * side), (route // 2) % side)
                slot = jnp.where(core == 0, at_y * side + at_z, at_z * side + at_y)
                slot = jnp.where(route % 2 == core, slot, slots)
                slot_ref[(half * blocks + k) * TOP + t] = slot

                @pl.when(slot < slots)
                def _(slot=slot, value=value):
                    total = out_ref[slot].astype(jnp.float32) + value
                    out_ref[slot] = total.astype(out_ref.dtype)


def gather_kernel(slot_ref, dual_ref, own_ref, other_ref):
    slots = dual_ref.shape[0]
    blocks = own_ref.shape[1] // PIX
    for half, ref in ((1, other_ref), (0, own_ref)):
        for k in range(blocks):
            total = jnp.zeros(dual_ref.shape[1:], jnp.float32)
            for t in range(TOP):
                slot = slot_ref[(half * blocks + k) * TOP + t]
                held = dual_ref[jnp.minimum(slot, slots - 1)].astype(jnp.float32)
                total = total + jnp.where(slot < slots, held, 0.0)
            ref[:, k * PIX : (k + 1) * PIX] = total.astype(ref.dtype)


def stencil_kernel(
    flat_ref, taps_ref, before_ref, after_ref, ws_ref, wc_ref, local_ref, up_ref, down_ref, mixed_ref
):
    full, columns = flat_ref.shape
    channels = ws_ref.shape[0]
    half = columns // 2
    column = lax.broadcasted_iota(jnp.int32, (SUB, half), 1)
    first, last = (column == 0, column == half - 1)

    def step(g, carry):
        rows = pl.ds(pl.multiple_of(g * SUB, SUB), SUB)
        taps = taps_ref[rows, :]
        before = before_ref[rows, :].astype(jnp.float32)
        after = after_ref[rows, :].astype(jnp.float32)

        def weight(a, e):
            n = a * 3 + e
            return taps[:, n : n + 1]

        views = []
        for i in range(2):
            x = flat_ref[rows, i * half : (i + 1) * half].astype(jnp.float32)
            left = jnp.where(first, before[:, PIX - 1 - i : PIX - i], pltpu.roll(x, 1, 1))
            right = jnp.where(last, after[:, i : i + 1], pltpu.roll(x, half - 1, 1))
            views.append((left, x, right))

        def row_sum(a, i):
            left, x, right = views[i]
            return weight(a, 0) * left + weight(a, 1) * x + weight(a, 2) * right

        parts = (
            row_sum(1, 0) + row_sum(2, 1),
            row_sum(0, 0) + row_sum(1, 1),
            row_sum(2, 0),
            row_sum(0, 1),
        )
        for n, part in enumerate(parts):
            mixed_ref[rows, n * half : (n + 1) * half] = part.astype(jnp.bfloat16)
        return carry

    lax.fori_loop(0, full // SUB, step, 0)
    local_ref[...] = across(ws_ref[...], flat_ref[:channels, :], ((0,), (0,))) + across(
        wc_ref[...], mixed_ref[:channels, :columns], ((0,), (0,))
    )
    sent = across(wc_ref[...], mixed_ref[:channels, columns:], ((0,), (0,))).astype(jnp.bfloat16)
    up_ref[...] = sent[:, :half]
    down_ref[...] = sent[:, half:]


def update_kernel(base_ref, own_ref, other_ref, lift_ref, wo_ref, flat_ref, out_ref, hidden_ref):
    half = flat_ref.shape[1] // 2

    @pl.when(pl.program_id(0) == 0)
    def _():
        back = (own_ref[...] + other_ref[...].astype(jnp.float32)).astype(jnp.bfloat16)
        pre = base_ref[...] + across(lift_ref[...], back, ((1,), (0,)))
        hidden_ref[...] = jax.nn.gelu(pre).astype(jnp.bfloat16)

    after = across(wo_ref[...], hidden_ref[...], ((1,), (0,))) + flat_ref[...].astype(jnp.float32)
    after = after.astype(out_ref.dtype)
    for i in range(2):
        out_ref[:, i, :] = after[:, i * half : (i + 1) * half]


def like(shape, dtype):
    return jax.ShapeDtypeStruct(shape, dtype)


def on_device(
    state,
    kernel,
    w_state,
    w_conv,
    w_adj,
    bias_in,
    w_out,
    obs_op,
    observations,
    obs_mask,
    dual_in,
    dual_res,
    dual_prev,
    dual_bias,
    dual_out_w,
    footprint,
):
    channels, lat_rows, lon_cols = state.shape
    radiance = obs_op.shape[0]
    hid = w_state.shape[0]
    owners = lax.axis_size("band")
    lon_count = lax.axis_size("lon")
    nblocks = lat_rows * lon_cols // PIX
    columns = lat_rows * lon_cols
    full = -(-channels // SUB) * SUB
    extra = full - channels
    side = math.isqrt(owners // 2)
    slots = side * side
    device = [[[(y * side + z) * 2 + c for c in range(2)] for z in range(side)] for y in range(side)]
    by_y = [[[device[y][z][c] for y in range(side)] for z in range(side)] for c in range(2)]
    by_z = [[[device[y][z][c] for z in range(side)] for y in range(side)] for c in range(2)]
    first, second = (by_y[0] + by_z[1], by_z[0] + by_y[1])
    swap = [(i, i ^ 1) for i in range(owners)]
    core = lax.axis_index("band") % 2

    def exchange(value, groups):
        return lax.all_to_all(
            value, "band", split_axis=0, concat_axis=0, axis_index_groups=groups, tiled=True
        )

    routes = footprint.reshape(nblocks * TOP)
    routes_other = lax.ppermute(routes, "band", swap)

    flat = jnp.pad(state, ((0, extra), (0, 0), (0, 0))).reshape(full, columns)
    projected = jnp.dot(
        obs_op, flat[:channels], preferred_element_type=jnp.float32
    ).astype(jnp.bfloat16)
    projected_other = lax.ppermute(projected, "band", swap)
    shares, slot = pl.pallas_call(
        scatter_kernel,
        out_shape=(
            like((slots, radiance, PIX), jnp.bfloat16),
            like((2 * nblocks * TOP,), jnp.int32),
        ),
        in_specs=[SMEM, SMEM, SMEM, VMEM, VMEM],
        out_specs=(VMEM, SMEM),
        name="scatter",
    )(core.reshape(1), routes, routes_other, projected, projected_other)
    arrived = exchange(shares, first)

    flat_late, _ = lax.optimization_barrier((flat, slot))
    up = [(i, (i + 1) % lon_count) for i in range(lon_count)]
    down = [(j, i) for i, j in up]
    lanes = [0, lon_cols // PIX, lon_cols // PIX - 1, columns // PIX - 1]
    initial, final = pl.pallas_call(
        edges_kernel,
        out_shape=(like((full, PIX), jnp.bfloat16),) * 2,
        grid=(1,),
        in_specs=[pl.BlockSpec((full, PIX), lambda i, n=n: (0, n)) for n in lanes],
        out_specs=(pl.BlockSpec((full, PIX), lambda i: (0, 0)),) * 2,
        name="edges",
    )(flat_late, flat_late, flat_late, flat_late)
    before = lax.ppermute(final, "lon", up)
    after = lax.ppermute(initial, "lon", down)
    taps = jnp.pad(kernel.reshape(channels, 9), ((0, extra), (0, 0)))
    local, to_up, to_down = pl.pallas_call(
        stencil_kernel,
        out_shape=(
            like((hid, columns), jnp.float32),
            like((hid, lon_cols), jnp.bfloat16),
            like((hid, lon_cols), jnp.bfloat16),
        ),
        in_specs=[VMEM] * 6,
        out_specs=(VMEM,) * 3,
        scratch_shapes=[pltpu.VMEM((full, 2 * columns), jnp.bfloat16)],
        name="stencil",
    )(flat_late, taps, before, after, w_state.T, w_conv.T)
    lift = across(w_adj, obs_op, ((1,), (1,))).astype(jnp.bfloat16)
    arrived, local, to_up, to_down, lift = lax.optimization_barrier(
        (arrived, local, to_up, to_down, lift)
    )

    summed = jnp.sum(
        arrived.reshape(side, side, radiance, PIX), axis=0, dtype=jnp.float32
    ).astype(jnp.bfloat16)
    evolved = jnp.sum(exchange(summed, second), axis=0, dtype=jnp.float32)

    observed = observations.reshape(radiance, PIX)
    valid = obs_mask.reshape(radiance, PIX)
    dual_now = dual_in.reshape(radiance, PIX)
    departure = jnp.where(valid == 1, evolved - observed, 0.0).astype(jnp.bfloat16)
    pre_dual = jnp.dot(dual_res, departure, preferred_element_type=jnp.float32)
    pre_dual = pre_dual + jnp.dot(dual_prev, dual_now, preferred_element_type=jnp.float32)
    dual_hidden = jax.nn.gelu(pre_dual + dual_bias[:, None]).astype(jnp.bfloat16)
    dual_new = (
        dual_now.astype(jnp.float32)
        + jnp.dot(dual_out_w, dual_hidden, preferred_element_type=jnp.float32)
    ).astype(jnp.bfloat16)

    column_of = exchange(jnp.broadcast_to(dual_new, (side, radiance, PIX)), second)
    spread = jnp.broadcast_to(column_of, (side, side, radiance, PIX)).reshape(slots, radiance, PIX)
    spread, to_up, to_down = lax.optimization_barrier((spread, to_up, to_down))
    all_of = exchange(spread, first)
    onward = [(i, i + 1) for i in range(owners - 1)]
    above = lax.ppermute(to_down, "band", onward)
    below = lax.ppermute(to_up, "band", [(j, i) for i, j in onward])
    base = local + jnp.concatenate([above, below], axis=1).astype(jnp.float32) + bias_in[:, None]
    all_of, base = lax.optimization_barrier((all_of, base))
    back_own, back_other = pl.pallas_call(
        gather_kernel,
        out_shape=(
            like((radiance, columns), jnp.float32),
            like((radiance, columns), jnp.bfloat16),
        ),
        in_specs=[SMEM, VMEM],
        out_specs=(VMEM, VMEM),
        name="gather",
    )(slot, all_of)
    back_from = lax.ppermute(back_other, "band", swap)

    def whole(*shape):
        return pl.BlockSpec(shape, lambda i: (0, 0))

    state_out = pl.pallas_call(
        update_kernel,
        out_shape=like(state.shape, jnp.bfloat16),
        grid=(-(-channels // CHUNK),),
        in_specs=[
            whole(hid, columns),
            whole(radiance, columns),
            whole(radiance, columns),
            whole(hid, radiance),
            pl.BlockSpec((CHUNK, hid), lambda i: (i, 0)),
            pl.BlockSpec((CHUNK, columns), lambda i: (i, 0)),
        ],
        out_specs=pl.BlockSpec((CHUNK, lat_rows, lon_cols), lambda i: (i, 0, 0)),
        scratch_shapes=[pltpu.VMEM((hid, columns), jnp.bfloat16)],
        name="update",
    )(base, back_own, back_from, lift, w_out, flat)
    return (state_out, dual_new.reshape(radiance, 1, PIX))


def solution(mesh):
    in_specs = (
        P(None, "band", "lon"),
        P(),
        P(),
        P(),
        P(),
        P(),
        P(),
        P(),
        P(None, "band", "lon"),
        P(None, "band", "lon"),
        P(None, "band", "lon"),
        P(),
        P(),
        P(),
        P(),
        P("band", "lon", None, None),
    )
    out_specs = (P(None, "band", "lon"), P(None, "band", "lon"))
    return jax.shard_map(
        on_device, mesh=mesh, in_specs=in_specs, out_specs=out_specs, check_vma=False
    )
```

time: 142 us -> 137 us (0.965)
  blocking collectives: 39.1 us -> 11 us
  waiting for transfers between devices: 9.84 us -> 28.4 us
  local copies, waits for them, and re-layouts: 25.2 us -> 12.5 us
  starting transfers between devices: 39.4 us -> 51.3 us
  other arithmetic: 1.65 us -> 3.59 us
  Pallas kernels: 24.2 us -> 25.8 us
    all_to_all x2 -> x1, blocking collectives: 39.1 us -> 11 us  [exchange(): lax.all_to_all(value, 'band', split_axis=0, concat_axis=0, axis_index_gro...]
    ppermute x1, waiting for transfers between devices: 0.01 us -> 11.8 us  [on_device(): above = lax.ppermute(to_down, 'band', onward)]
    all_to_all x2 -> x3, starting transfers between devices: 11.2 us -> 18.1 us  [exchange(): lax.all_to_all(value, 'band', split_axis=0, concat_axis=0, axis_index_gro...]
    optimization_barrier x1 -> x0, local copies, waits for them, and re-layouts: 6.76 us -> none  [on_device(): lax.optimization_barrier((state, flat, projected_other))]
    unnamed x44 -> x52, local copies, waits for them, and re-layouts: 3.21 us -> 8.71 us
    ppermute x1, starting transfers between devices: 2.23 us -> 7.48 us  [on_device(): back_from = lax.ppermute(back_other, 'band', swap)]
    ppermute x1, starting transfers between devices: 6.68 us -> 1.92 us  [on_device(): below = lax.ppermute(to_up, 'band', [(j, i) for i, j in onward])]
    ppermute x1, starting transfers between devices: 2.1 us -> 6.65 us  [on_device(): above = lax.ppermute(to_down, 'band', onward)]
  transfers between devices with their start and end apart: 9 -> 10, of which waited for: 3 -> 8; matrix products, arithmetic and copies ran while one was open for 10% -> 5% of each run, Pallas kernels for 10% -> 10%
where the time goes in v2:
time: 137 us; the launch traced here: 136 us
  starting transfers between devices  51.3 us (37%)
  waiting for transfers between devices  28.4 us (21%)
  Pallas kernels  25.8 us (19%)
  local copies, waits for them, and re-layouts  12.5 us (9%)
  blocking collectives  11 us (8%)
  other arithmetic  3.59 us (3%)
  matrix products  2.07 us (2%)
    all_to_all x3, starting transfers between devices, exchange(): lax.all_to_all(value, 'band', split_axis=0, concat_axis=0, axis_index_gro...  18.1 us
    ppermute x1, waiting for transfers between devices, on_device(): above = lax.ppermute(to_down, 'band', onward)  11.8 us
    pallas_call x1, Pallas kernels, on_device(): pl.pallas_call(stencil_kernel, out_shape=(like((hid, columns), jnp.float3...  11.5 us
    all_to_all x1, blocking collectives, exchange(): lax.all_to_all(value, 'band', split_axis=0, concat_axis=0, axis_index_gro...  11 us
    all_to_all x3, waiting for transfers between devices, exchange(): lax.all_to_all(value, 'band', split_axis=0, concat_axis=0, axis_index_gro...  8.76 us
    ppermute x1, starting transfers between devices, on_device(): projected_other = lax.ppermute(projected, 'band', swap)  8.75 us
    unnamed x52, local copies, waits for them, and re-layouts  8.71 us
    ppermute x1, starting transfers between devices, on_device(): back_from = lax.ppermute(back_other, 'band', swap)  7.48 us
  transfers between devices with their start and end apart: 10, of which 8 were waited for; matrix products, arithmetic and copies ran while one was open for 5% of the time, Pallas kernels for 10%

profile of v2, /device:TPU:1, one launch (start us, length us, event | category | flops | bytes accessed | tf_op | source)
XLA Modules:
  0.0 135.7 jit_solution(1798303843709521356)
XLA Ops:
  0.6 0.0 copy-start
  0.6 2.8 %pad.12 = bf16[824,2,512]{2,1,0:T(2,128)(2,1)S(1)} pad(bf16[822,2,512]{2,1,0:T(2,128)(2,1)} %param.16, bf16[]{:T(256)} %constant.29.clone.1), padding=0_2x0_0x0_0 | pad | bytes 3371010
  3.4 0.0 copy-start.5
  3.5 0.4 copy.33
  3.9 0.0 copy-start.15
  3.9 0.5 copy-done.5
  4.4 0.5 convolution_convert_fusion.own_ref
  4.9 0.0 copy-start.4
  4.9 8.7 %collective-permute-start.1 = (bf16[96,1024]{1,0:T(8,128)(2,1)S(1)}, bf16[96,1024]{1,0:T(8,128)(2,1)S(1)}, u32[]{:S(2)}, u32[]{:S(2)}) collective-permute-start(bf16[96,1024]{1,0:T(8,128)(2,1)S(1)} %convolution_convert_fusion.own_ref), channel_id=1, source_target_pairs={{0,4},{4,0},{8,12},{12,8},{16,20},{20,16},{24,28},{28,24},{32,36},... | collective-permute-start | bytes 589832 | tf_op jit(solution)/shard_map/ppermute | solution.py:191
  13.7 0.0 copy-done.15
  13.7 0.1 copy.27
  13.8 0.1 reshape.39.own_route_ref
  13.9 1.9 %collective-permute-start = (s32[32]{0:T(128)S(1)}, s32[32]{0:T(128)S(1)}, u32[]{:S(2)}, u32[]{:S(2)}) collective-permute-start(s32[32]{0:T(128)S(1)} %reshape.39.own_route_ref), channel_id=1, source_target_pairs={{0,4},{4,0},{8,12},{12,8},{16,20},{20,16},{24,28},{28,24},{32,36},... | collective-permute-start | bytes 392 | tf_op jit(solution)/shard_map/ppermute | solution.py:185
  15.8 1.1 collective-permute-done.other_route_ref
  16.9 0.0 collective-permute-done.1.other_ref
  16.9 0.5 copy-done.17
  17.4 0.2 copy-done.9
  17.6 4.1 %scatter.1 = (bf16[64,96,128]{2,1,0:T(8,128)(2,1)}, s32[64]{0:T(128)}) custom-call(s32[1]{0:T(128)} %bitcast.3.core_ref, s32[32]{0:T(128)} %copy-done.14, s32[32]{0:T(128)} %copy-done.17, bf16[96,1024]{1,0:T(8,128)(2,1)} %copy-done.4, bf16[96,1024]{1,0:T(8,128)(2,1)} %copy-done.9), custom_call_target="tpu_custom_call" | custom-call | tf_op jit(solution)/shard_map/scatter/pallas_call | solution.py:192
  21.7 4.7 %all-to-all-start = ((bf16[64,96,128]{2,1,0:T(8,128)(2,1)}), bf16[64,96,128]{2,1,0:T(8,128)(2,1)}, u32[]{:S(2)}, u32[]{:S(2)}) async-start(bf16[64,96,128]{2,1,0:T(8,128)(2,1)} %get-tuple-element.22), calls=%async_computation | async-start | bytes 3145728 | tf_op jit(solution)/shard_map/all_to_all | solution.py:180
  26.4 1.3 pad.8
  27.7 0.0 copy-start.11
  27.7 1.7 %copy.34 = bf16[104,8,2,512]{3,1,2,0:T(8,128)(2,1)} copy(bf16[104,8,2,512]{3,2,1,0:T(2,128)(2,1)S(1)} %bitcast.56) | data formatting | bytes 3407872
  29.4 0.2 copy.28
  29.6 0.8 pad.9.taps_ref
  30.4 2.2 %edges.1 = (bf16[832,128]{1,0:T(8,128)(2,1)}, bf16[832,128]{1,0:T(8,128)(2,1)}) custom-call(bf16[832,1024]{1,0:T(8,128)(2,1)} %bitcast.50, bf16[832,1024]{1,0:T(8,128)(2,1)} %bitcast.51, bf16[832,1024]{1,0:T(8,128)(2,1)} %bitcast.52, bf16[832,1024]{1,0:T(8,128)(2,1)} %bitcast.53), custom_call_target="tpu_custom_call" | custom-call | tf_op jit(solution)/shard_map/edges/pallas_call | solution.py:208
  32.6 3.1 %collective-permute-start.2 = (bf16[832,128]{1,0:T(8,128)(2,1)}, bf16[832,128]{1,0:T(8,128)(2,1)S(1)}, u32[]{:S(2)}, u32[]{:S(2)}) collective-permute-start(bf16[832,128]{1,0:T(8,128)(2,1)} %get-tuple-element.25), channel_id=1, source_target_pairs={{0,1},{1,2},{2,3},{3,0},{4,5},{5,6},{6,7},{7,4},{8,9},{9,10},{10,1... | collective-permute-start | bytes 638984 | tf_op jit(solution)/shard_map/ppermute | solution.py:216
  35.7 3.4 %collective-permute-start.3 = (bf16[832,128]{1,0:T(8,128)(2,1)}, bf16[832,128]{1,0:T(8,128)(2,1)S(1)}, u32[]{:S(2)}, u32[]{:S(2)}) collective-permute-start(bf16[832,128]{1,0:T(8,128)(2,1)} %get-tuple-element.26), channel_id=1, source_target_pairs={{1,0},{2,1},{3,2},{0,3},{5,4},{6,5},{7,6},{4,7},{9,8},{10,9},{11,1... | collective-permute-start | bytes 638984 | tf_op jit(solution)/shard_map/ppermute | solution.py:217
  39.1 0.9 convolution_convert_fusion.1.lift_ref
  40.0 3.0 %collective-permute-done.2.before_ref = bf16[832,128]{1,0:T(8,128)(2,1)S(1)} collective-permute-done((bf16[832,128]{1,0:T(8,128)(2,1)}, bf16[832,128]{1,0:T(8,128)(2,1)S(1)}, u32[]{:S(2)}, u32[]{:S(2)}) %collective-permute-start.2) | collective-permute-done | bytes 213024 | tf_op jit(solution)/shard_map/ppermute | solution.py:216
  43.0 0.9 collective-permute-done.3.after_ref
  44.0 0.7 copy-done.7
  44.6 11.5 %stencil.1 = (f32[256,1024]{1,0:T(8,128)}, bf16[256,512]{1,0:T(8,128)(2,1)}, bf16[256,512]{1,0:T(8,128)(2,1)}) custom-call(bf16[832,1024]{1,0:T(8,128)(2,1)} %bitcast.54, f32[832,9]{1,0:T(8,128)} %pad.9.taps_ref, bf16[832,128]{1,0:T(8,128)(2,1)} %copy-done.6, bf16[832,128]{1,0:T(8,128)(2,1)} %copy-done.7, bf16[822,256]{1,0:T(8,128)(2,1)} %bitcast.60, ...), custom_call_target="tpu_custom_call" | custom-call | tf_op jit(solution)/shard_map/stencil/pallas_call | solution.py:219
  56.2 0.0 copy-start.20
  56.2 0.0 copy-start.21
  56.2 0.0 copy-start.22
  56.2 0.0 copy-start.23
  56.2 0.0 all-to-all-done
  56.2 2.4 %reduce_sum.21 = bf16[8,96,128]{2,1,0:T(8,128)(2,1)} reduce(bf16[8,8,96,128]{3,2,1,0:T(8,128)(2,1)} %bitcast.6, bf16[]{:T(256)} %constant.29.clone.1), dimensions={0}, to_apply=%region_0.1 | reduce | flops 688128 | bytes 1769474 | tf_op jit(solution)/shard_map/reduce_sum | solution.py:236
  58.6 7.1 %all-to-all-start.1 = ((bf16[8,96,128]{2,1,0:T(8,128)(2,1)}), bf16[8,96,128]{2,1,0:T(8,128)(2,1)S(1)}, u32[]{:S(2)}, u32[]{:S(2)}) async-start(bf16[8,96,128]{2,1,0:T(8,128)(2,1)} %reduce_sum.21), calls=%async_computation.1 | async-start | bytes 393216 | tf_op jit(solution)/shard_map/all_to_all | solution.py:180
  65.7 0.0 copy-done.12
  65.7 0.2 fusion.17
  66.0 8.4 %all-to-all-done.1 = bf16[8,96,128]{2,1,0:T(8,128)(2,1)S(1)} async-done(((bf16[8,96,128]{2,1,0:T(8,128)(2,1)}), bf16[8,96,128]{2,1,0:T(8,128)(2,1)S(1)}, u32[]{:S(2)}, u32[]{:S(2)}) %all-to-all-start.1) | async-done | bytes 196640 | tf_op jit(solution)/shard_map/all_to_all | solution.py:180
  74.4 0.0 copy-done.19
  74.4 0.0 copy-done.20
  74.4 0.0 copy-done.21
  74.4 0.0 copy-done.22
  74.4 0.0 copy-done.23
  74.4 0.4 fusion.3
  74.8 0.0 copy-start.13
  74.9 11.0 %all_to_all.20 = bf16[8,96,128]{2,1,0:T(8,128)(2,1)S(1)} all-to-all(bf16[8,96,128]{2,1,0:T(8,128)(2,1)S(1)} %broadcast_in_dim.13), channel_id=1, replica_groups={{0,8,16,24,32,40,48,56},{64,72,80,88,96,104,112,120},{128,136,144,152,1..., dimensions={0} | all-to-all | bytes 393216 | tf_op jit(solution)/shard_map/all_to_all | solution.py:180
  85.9 1.4 %broadcast_in_dim.14 = bf16[8,8,96,128]{3,2,1,0:T(8,128)(2,1)} broadcast(bf16[8,96,128]{2,1,0:T(8,128)(2,1)S(1)} %all_to_all.20), dimensions={1,2,3} | broadcast | bytes 1769472 | tf_op jit(solution)/shard_map/broadcast_in_dim | solution.py:254
  87.3 6.3 %all-to-all-start.3 = ((bf16[64,96,128]{2,1,0:T(8,128)(2,1)}), bf16[64,96,128]{2,1,0:T(8,128)(2,1)S(1)}, u32[]{:S(2)}, u32[]{:S(2)}) async-start(bf16[64,96,128]{2,1,0:T(8,128)(2,1)} %bitcast.59), calls=%async_computation.3 | async-start | bytes 3145728 | tf_op jit(solution)/shard_map/all_to_all | solution.py:180
  93.6 6.7 %collective-permute-start.4 = (bf16[256,512]{1,0:T(8,128)(2,1)}, bf16[256,512]{1,0:T(8,128)(2,1)S(1)}, u32[]{:S(2)}, u32[]{:S(2)}) collective-permute-start(bf16[256,512]{1,0:T(8,128)(2,1)} %get-tuple-element.35), channel_id=1, source_target_pairs={{0,4},{4,8},{8,12},{12,16},{16,20},{20,24},{24,28},{28,32},{32,36}... | collective-permute-start | bytes 786440 | tf_op jit(solution)/shard_map/ppermute | solution.py:258
  100.3 1.9 %collective-permute-start.5 = (bf16[256,512]{1,0:T(8,128)(2,1)S(1)}, bf16[256,512]{1,0:T(8,128)(2,1)S(1)}, u32[]{:S(2)}, u32[]{:S(2)}) collective-permute-start(bf16[256,512]{1,0:T(8,128)(2,1)S(1)} %copy-done.18), channel_id=1, source_target_pairs={{4,0},{8,4},{12,8},{16,12},{20,16},{24,20},{28,24},{32,28},{36,32}... | collective-permute-start | bytes 786440 | tf_op jit(solution)/shard_map/ppermute | solution.py:259
  102.2 11.8 %collective-permute-done.4 = bf16[256,512]{1,0:T(8,128)(2,1)S(1)} collective-permute-done((bf16[256,512]{1,0:T(8,128)(2,1)}, bf16[256,512]{1,0:T(8,128)(2,1)S(1)}, u32[]{:S(2)}, u32[]{:S(2)}) %collective-permute-start.4) | collective-permute-done | bytes 262176 | tf_op jit(solution)/shard_map/ppermute | solution.py:258
  114.0 1.7 %collective-permute-done.5 = bf16[256,512]{1,0:T(8,128)(2,1)S(1)} collective-permute-done((bf16[256,512]{1,0:T(8,128)(2,1)S(1)}, bf16[256,512]{1,0:T(8,128)(2,1)S(1)}, u32[]{:S(2)}, u32[]{:S(2)}) %collective-permute-start.5) | collective-permute-done | bytes 262176 | tf_op jit(solution)/shard_map/ppermute | solution.py:259
  115.6 1.2 add_add_fusion.base_ref
  116.8 0.4 all-to-all-done.3.dual_ref
  117.1 1.1 copy-done.2
  118.3 2.5 %gather.1 = (f32[96,1024]{1,0:T(8,128)}, bf16[96,1024]{1,0:T(8,128)(2,1)}) custom-call(s32[64]{0:T(128)} %get-tuple-element.23.slot_ref, bf16[64,96,128]{2,1,0:T(8,128)(2,1)} %copy-done.2), custom_call_target="tpu_custom_call" | custom-call | tf_op jit(solution)/shard_map/gather/pallas_call | solution.py:262
  120.8 7.5 %collective-permute-start.6 = (bf16[96,1024]{1,0:T(8,128)(2,1)}, bf16[96,1024]{1,0:T(8,128)(2,1)S(1)}, u32[]{:S(2)}, u32[]{:S(2)}) collective-permute-start(bf16[96,1024]{1,0:T(8,128)(2,1)} %get-tuple-element.40), channel_id=1, source_target_pairs={{0,4},{4,0},{8,12},{12,8},{16,20},{20,16},{24,28},{28,24},{32,36},... | collective-permute-start | bytes 589832 | tf_op jit(solution)/shard_map/ppermute | solution.py:272
  128.3 1.3 collective-permute-done.6.other_ref
  129.5 0.7 copy-done.8
  130.2 5.5 %update.1 = bf16[822,2,512]{2,1,0:T(2,128)(2,1)} custom-call(f32[256,1024]{1,0:T(8,128)} %add_add_fusion.base_ref, f32[96,1024]{1,0:T(8,128)} %get-tuple-element.39.own_ref, bf16[96,1024]{1,0:T(8,128)(2,1)} %copy-done.8, bf16[256,96]{1,0:T(8,128)(2,1)} %convolution_convert_fusion.1.lift_ref, bf16[822,256]{1,0:T(8,128)(2,1)} %wo_ref.1, bf16[832,1024]{1,0:T(8,128)(2,1)} %bitcast.55), custom_call_target="tpu_custom_call" | custom-call | tf_op jit(solution)/shard_map/update/pallas_call | solution.py:277
  (28 shorter events, 0.1 us)
Async XLA Ops:
  0.6 38.5 %copy-start = (bf16[256,822]{0,1:T(8,128)(2,1)S(1)}, bf16[256,822]{0,1:T(8,128)(2,1)}, u32[]{:S(2)}) copy-start(bf16[256,822]{0,1:T(8,128)(2,1)} %param.20) | copy-start | bytes 1262596
  3.4 0.9 copy-start.5
  3.9 9.8 %copy-start.15 = (s32[1,1,8,4]{2,3,1,0:T(4,128)S(1)}, s32[1,1,8,4]{2,3,1,0:T(4,128)}, u32[]{:S(2)}) copy-start(s32[1,1,8,4]{2,3,1,0:T(4,128)} %param.31) | copy-start | bytes 388
  4.9 12.0 %copy-start.4 = (bf16[96,1024]{1,0:T(8,128)(2,1)}, bf16[96,1024]{1,0:T(8,128)(2,1)S(1)}, u32[]{:S(2)}) copy-start(bf16[96,1024]{1,0:T(8,128)(2,1)S(1)} %convolution_convert_fusion.own_ref) | copy-start | bytes 589828
  4.9 12.0 %collective-permute-start.1 = (bf16[96,1024]{1,0:T(8,128)(2,1)S(1)}, bf16[96,1024]{1,0:T(8,128)(2,1)S(1)}, u32[]{:S(2)}, u32[]{:S(2)}) collective-permute-start(bf16[96,1024]{1,0:T(8,128)(2,1)S(1)} %convolution_convert_fusion.own_ref), channel_id=1, source_target_pairs={{0,4},{4,0},{8,12},{12,8},{16,20},{20,16},{24,28},{28,24},{32,36},... | collective-permute-start | bytes 589832 | tf_op jit(solution)/shard_map/ppermute | solution.py:191
  13.9 3.1 %copy-start.14 = (s32[32]{0:T(128)}, s32[32]{0:T(128)S(1)}, u32[]{:S(2)}) copy-start(s32[32]{0:T(128)S(1)} %reshape.39.own_route_ref) | copy-start | bytes 388
  13.9 3.0 %collective-permute-start = (s32[32]{0:T(128)S(1)}, s32[32]{0:T(128)S(1)}, u32[]{:S(2)}, u32[]{:S(2)}) collective-permute-start(s32[32]{0:T(128)S(1)} %reshape.39.own_route_ref), channel_id=1, source_target_pairs={{0,4},{4,0},{8,12},{12,8},{16,20},{20,16},{24,28},{28,24},{32,36},... | collective-permute-start | bytes 392 | tf_op jit(solution)/shard_map/ppermute | solution.py:185
  16.9 0.5 copy-start.17
  16.9 0.7 copy-start.9
  17.6 8.8 %copy-start.1 = (bf16[822,2,512]{2,1,0:T(2,128)(2,1)S(1)}, bf16[822,2,512]{2,1,0:T(2,128)(2,1)}, u32[]{:S(2)}) copy-start(bf16[822,2,512]{2,1,0:T(2,128)(2,1)} %param.16) | copy-start | bytes 5050372
  21.7 34.5 %all-to-all-start = ((bf16[64,96,128]{2,1,0:T(8,128)(2,1)}), bf16[64,96,128]{2,1,0:T(8,128)(2,1)}, u32[]{:S(2)}, u32[]{:S(2)}) async-start(bf16[64,96,128]{2,1,0:T(8,128)(2,1)} %get-tuple-element.22), calls=%async_computation | async-start | bytes 3145728 | tf_op jit(solution)/shard_map/all_to_all | solution.py:180
  27.7 1.7 %copy-start.11 = (f32[822,3,3]{0,2,1:T(4,128)S(1)}, f32[822,3,3]{0,2,1:T(4,128)}, u32[]{:S(2)}) copy-start(f32[822,3,3]{0,2,1:T(4,128)} %param.17) | copy-start | bytes 88780
  32.6 10.4 %collective-permute-start.2 = (bf16[832,128]{1,0:T(8,128)(2,1)}, bf16[832,128]{1,0:T(8,128)(2,1)S(1)}, u32[]{:S(2)}, u32[]{:S(2)}) collective-permute-start(bf16[832,128]{1,0:T(8,128)(2,1)} %get-tuple-element.25), channel_id=1, source_target_pairs={{0,1},{1,2},{2,3},{3,0},{4,5},{5,6},{6,7},{7,4},{8,9},{9,10},{10,1... | collective-permute-start | bytes 638984 | tf_op jit(solution)/shard_map/ppermute | solution.py:216
  35.7 8.3 %collective-permute-start.3 = (bf16[832,128]{1,0:T(8,128)(2,1)}, bf16[832,128]{1,0:T(8,128)(2,1)S(1)}, u32[]{:S(2)}, u32[]{:S(2)}) collective-permute-start(bf16[832,128]{1,0:T(8,128)(2,1)} %get-tuple-element.26), channel_id=1, source_target_pairs={{1,0},{2,1},{3,2},{0,3},{5,4},{6,5},{7,6},{4,7},{9,8},{10,9},{11,1... | collective-permute-start | bytes 638984 | tf_op jit(solution)/shard_map/ppermute | solution.py:217
  43.0 0.9 copy-start.6
  43.9 0.7 copy-start.7
  56.2 9.6 %copy-start.10 = (bf16[256,96]{0,1:T(8,128)(2,1)S(1)}, bf16[256,96]{0,1:T(8,128)(2,1)}, u32[]{:S(2)}) copy-start(bf16[256,96]{0,1:T(8,128)(2,1)} %param.28) | copy-start | bytes 147460
  56.2 9.6 %copy-start.12 = (bf16[96,1,128]{2,0,1:T(8,128)(2,1)S(1)}, bf16[96,1,128]{2,0,1:T(8,128)(2,1)}, u32[]{:S(2)}) copy-start(bf16[96,1,128]{2,0,1:T(8,128)(2,1)} %param.26) | copy-start | bytes 73732
  56.2 18.2 %copy-start.19 = (bf16[96,256]{1,0:T(8,128)(2,1)S(1)}, bf16[96,256]{1,0:T(8,128)(2,1)}, u32[]{:S(2)}) copy-start(bf16[96,256]{1,0:T(8,128)(2,1)} %param.30) | copy-start | bytes 147460
  56.2 18.2 %copy-start.20 = (bf16[256,96]{0,1:T(8,128)(2,1)S(1)}, bf16[256,96]{0,1:T(8,128)(2,1)}, u32[]{:S(2)}) copy-start(bf16[256,96]{0,1:T(8,128)(2,1)} %param.27) | copy-start | bytes 147460
  56.2 18.2 %copy-start.21 = (f32[96,1,128]{2,1,0:T(1,128)S(1)}, f32[96,1,128]{2,1,0:T(1,128)}, u32[]{:S(2)}) copy-start(f32[96,1,128]{2,1,0:T(1,128)} %param.24) | copy-start | bytes 147460
  56.2 18.2 %copy-start.22 = (s32[96,1,128]{2,1,0:T(1,128)S(1)}, s32[96,1,128]{2,1,0:T(1,128)}, u32[]{:S(2)}) copy-start(s32[96,1,128]{2,1,0:T(1,128)} %param.25) | copy-start | bytes 147460
  56.2 18.2 %copy-start.23 = (f32[256]{0:T(256)S(1)}, f32[256]{0:T(256)}, u32[]{:S(2)}) copy-start(f32[256]{0:T(256)} %param.29) | copy-start | bytes 3076
  58.6 15.7 %all-to-all-start.1 = ((bf16[8,96,128]{2,1,0:T(8,128)(2,1)}), bf16[8,96,128]{2,1,0:T(8,128)(2,1)S(1)}, u32[]{:S(2)}, u32[]{:S(2)}) async-start(bf16[8,96,128]{2,1,0:T(8,128)(2,1)} %reduce_sum.21), calls=%async_computation.1 | async-start | bytes 393216 | tf_op jit(solution)/shard_map/all_to_all | solution.py:180
  74.8 12.5 %copy-start.13 = (bf16[96,128]{1,0:T(8,128)(2,1)}, bf16[96,128]{1,0:T(8,128)(2,1)S(1)}, u32[]{:S(2)}) copy-start(bf16[96,128]{1,0:T(8,128)(2,1)S(1)} %fusion.3) | copy-start | bytes 73732
  87.3 13.0 %copy-start.18 = (bf16[256,512]{1,0:T(8,128)(2,1)S(1)}, bf16[256,512]{1,0:T(8,128)(2,1)}, u32[]{:S(2)}) copy-start(bf16[256,512]{1,0:T(8,128)(2,1)} %get-tuple-element.36) | copy-start | bytes 786436
  87.3 28.3 %copy-start.3 = (f32[256,1024]{1,0:T(8,128)S(1)}, f32[256,1024]{1,0:T(8,128)}, u32[]{:S(2)}) copy-start(f32[256,1024]{1,0:T(8,128)} %get-tuple-element.34) | copy-start | bytes 3145732
  87.3 28.3 %copy-start.16 = (f32[256]{0:T(256)S(1)}, f32[256]{0:T(256)}, u32[]{:S(2)}) copy-start(f32[256]{0:T(256)} %param.21) | copy-start | bytes 3076
  87.3 29.8 %all-to-all-start.3 = ((bf16[64,96,128]{2,1,0:T(8,128)(2,1)}), bf16[64,96,128]{2,1,0:T(8,128)(2,1)S(1)}, u32[]{:S(2)}, u32[]{:S(2)}) async-start(bf16[64,96,128]{2,1,0:T(8,128)(2,1)} %bitcast.59), calls=%async_computation.3 | async-start | bytes 3145728 | tf_op jit(solution)/shard_map/all_to_all | solution.py:180
  93.6 20.4 %collective-permute-start.4 = (bf16[256,512]{1,0:T(8,128)(2,1)}, bf16[256,512]{1,0:T(8,128)(2,1)S(1)}, u32[]{:S(2)}, u32[]{:S(2)}) collective-permute-start(bf16[256,512]{1,0:T(8,128)(2,1)} %get-tuple-element.35), channel_id=1, source_target_pairs={{0,4},{4,8},{8,12},{12,16},{16,20},{20,24},{24,28},{28,32},{32,36}... | collective-permute-start | bytes 786440 | tf_op jit(solution)/shard_map/ppermute | solution.py:258
  100.3 15.3 %collective-permute-start.5 = (bf16[256,512]{1,0:T(8,128)(2,1)S(1)}, bf16[256,512]{1,0:T(8,128)(2,1)S(1)}, u32[]{:S(2)}, u32[]{:S(2)}) collective-permute-start(bf16[256,512]{1,0:T(8,128)(2,1)S(1)} %copy-done.18), channel_id=1, source_target_pairs={{4,0},{8,4},{12,8},{16,12},{20,16},{24,20},{28,24},{32,28},{36,32}... | collective-permute-start | bytes 786440 | tf_op jit(solution)/shard_map/ppermute | solution.py:259
  117.1 1.1 copy-start.2
  120.8 8.7 %collective-permute-start.6 = (bf16[96,1024]{1,0:T(8,128)(2,1)}, bf16[96,1024]{1,0:T(8,128)(2,1)S(1)}, u32[]{:S(2)}, u32[]{:S(2)}) collective-permute-start(bf16[96,1024]{1,0:T(8,128)(2,1)} %get-tuple-element.40), channel_id=1, source_target_pairs={{0,4},{4,0},{8,12},{12,8},{16,20},{20,16},{24,28},{28,24},{32,36},... | collective-permute-start | bytes 589832 | tf_op jit(solution)/shard_map/ppermute | solution.py:272
  129.5 0.7 copy-start.8

commit v3 on v2

v3 whole, which is shorter than its diff:
```python
import math

import jax
import jax.numpy as jnp
from jax import lax
from jax.experimental import pallas as pl
from jax.experimental.pallas import tpu as pltpu
from jax.sharding import PartitionSpec as P

PIX = 128
TOP = 4
SUB = 16
CHUNK = 144

VMEM = pl.BlockSpec(memory_space=pltpu.MemorySpace.VMEM)
HBM = pl.BlockSpec(memory_space=pltpu.MemorySpace.HBM)
SMEM = pl.BlockSpec(memory_space=pltpu.MemorySpace.SMEM)


def across(a, b, dims):
    return lax.dot_general(a, b, (dims, ((), ())), preferred_element_type=jnp.float32)


def edges_kernel(first0_ref, first1_ref, last0_ref, last1_ref, first_ref, last_ref):
    lane = lax.broadcasted_iota(jnp.int32, first_ref.shape, 1)

    def pair(own, other, turn, at):
        turned = pltpu.roll(other[...].astype(jnp.float32), turn, 1)
        return jnp.where(lane == at, own[...].astype(jnp.float32), turned).astype(jnp.bfloat16)

    first_ref[...] = pair(first0_ref, first1_ref, 1, 0)
    last_ref[...] = pair(last0_ref, last1_ref, PIX - 1, PIX - 1)


def scatter_kernel(
    core_ref, own_route_ref, own_ref, other_ref, out_ref, slot_ref, wide_ref, route_ref, sem
):
    slots = out_ref.shape[0]
    side = math.isqrt(slots)
    bits = side.bit_length() - 1
    blocks = own_ref.shape[1] // PIX
    radiance = out_ref.shape[1]
    core = core_ref[0]
    empty = jnp.zeros(out_ref.shape[1:], out_ref.dtype)
    wide_ref[...] = other_ref[radiance:, :PIX].astype(jnp.float32).astype(jnp.int32)
    copy = pltpu.make_async_copy(wide_ref, route_ref, sem)
    copy.start()

    def clear(i, carry):
        out_ref[i] = empty
        return carry

    lax.fori_loop(0, slots, clear, 0, unroll=8)

    def place(half, ref, k):
        value = ref[:radiance, k * PIX : (k + 1) * PIX].astype(jnp.float32)
        for t in range(TOP):
            n = k * TOP + t
            route = own_route_ref[n] if half == 0 else route_ref[0, n]
            at = lax.shift_right_logical(route, 1)
            turned = (at & (side - 1)) * side + lax.shift_right_logical(at, bits)
            slot = jnp.where(core == 0, at, turned)
            slot = jnp.where((route & 1) == core, slot, slots)
            slot_ref[half * blocks * TOP + n] = slot

            @pl.when(slot < slots)
            def _(slot=slot, value=value):
                total = out_ref[slot].astype(jnp.float32) + value
                out_ref[slot] = total.astype(out_ref.dtype)

    for k in range(blocks):
        place(0, own_ref, k)
    copy.wait()
    for k in range(blocks):
        place(1, other_ref, k)


def gather_kernel(slot_ref, dual_ref, own_ref, other_ref):
    slots = dual_ref.shape[0]
    blocks = own_ref.shape[1] // PIX
    for half, ref in ((1, other_ref), (0, own_ref)):
        for k in range(blocks):
            total = jnp.zeros(dual_ref.shape[1:], jnp.float32)
            for t in range(TOP):
                slot = slot_ref[(half * blocks + k) * TOP + t]
                held = dual_ref[jnp.minimum(slot, slots - 1)].astype(jnp.float32)
                total = total + jnp.where(slot < slots, held, 0.0)
            ref[:, k * PIX : (k + 1) * PIX] = total.astype(ref.dtype)


def sum_kernel(far_ref, out_ref, part_ref, total_ref, sems):
    count = far_ref.shape[0]
    copies = [pltpu.make_async_copy(far_ref.at[i], part_ref.at[i], sems.at[i]) for i in range(count)]
    for copy in copies:
        copy.start()
    for i in range(0, count, 2):
        copies[i].wait()
        copies[i + 1].wait()
        for j in range(out_ref.shape[0]):
            pair = part_ref[i, j].astype(jnp.float32) + part_ref[i + 1, j].astype(jnp.float32)
            if i > 0:
                pair = total_ref[j] + pair
            if i + 2 < count:
                total_ref[j] = pair
            else:
                out_ref[j] = pair.astype(out_ref.dtype)


def stencil_kernel(
    flat_ref, taps_ref, before_ref, after_ref, wc_ref, local_ref, up_ref, down_ref, mixed_ref
):
    channels, columns = flat_ref.shape
    half = columns // 2

    def piece(rows, count):
        column = lax.broadcasted_iota(jnp.int32, (count, half), 1)
        first, last = (column == 0, column == half - 1)
        taps = taps_ref[rows, :]
        before = before_ref[rows, :].astype(jnp.float32)
        after = after_ref[rows, :].astype(jnp.float32)

        def weight(a, e):
            n = a * 3 + e
            return taps[:, n : n + 1]

        views = []
        for i in range(2):
            x = flat_ref[rows, i * half : (i + 1) * half].astype(jnp.float32)
            left = jnp.where(first, before[:, PIX - 1 - i : PIX - i], pltpu.roll(x, 1, 1))
            right = jnp.where(last, after[:, i : i + 1], pltpu.roll(x, half - 1, 1))
            views.append((left, x, right))

        def row_sum(a, i):
            left, x, right = views[i]
            return weight(a, 0) * left + weight(a, 1) * x + weight(a, 2) * right

        parts = (
            row_sum(1, 0) + row_sum(2, 1),
            row_sum(0, 0) + row_sum(1, 1),
            row_sum(2, 0),
            row_sum(0, 1),
        )
        for n, part in enumerate(parts):
            mixed_ref[rows, n * half : (n + 1) * half] = part.astype(jnp.bfloat16)

    steps = channels // SUB

    def step(g, carry):
        piece(pl.ds(pl.multiple_of(g * SUB, SUB), SUB), SUB)
        return carry

    lax.fori_loop(0, steps, step, 0, unroll=3)
    if channels > steps * SUB:
        piece(slice(steps * SUB, channels), channels - steps * SUB)
    sent = across(wc_ref[...], mixed_ref[:, columns:], ((0,), (0,))).astype(jnp.bfloat16)
    up_ref[...] = sent[:, :half]
    down_ref[...] = sent[:, half:]
    local_ref[...] = across(wc_ref[...], mixed_ref[:, :columns], ((0,), (0,)))


def update_kernel(
    base_ref, own_ref, other_ref, lift_ref, wo_ref, flat_ref, far_ref, hidden_ref, out_ref, sems
):
    channels, columns = flat_ref.shape
    half = columns // 2
    back = (own_ref[...] + other_ref[...].astype(jnp.float32)).astype(jnp.bfloat16)
    pre = base_ref[...] + across(lift_ref[...], back, ((1,), (0,)))
    hidden_ref[...] = jax.nn.gelu(pre).astype(jnp.bfloat16)
    copies = []
    for n, at in enumerate(range(0, channels, CHUNK)):
        rows = slice(at, min(at + CHUNK, channels))
        after = across(wo_ref[rows, :], hidden_ref[...], ((1,), (0,)))
        after = (after + flat_ref[rows, :].astype(jnp.float32)).astype(out_ref.dtype)
        for i in range(2):
            out_ref[rows, i, :] = after[:, i * half : (i + 1) * half]
        part = pl.ds(rows.start, rows.stop - rows.start)
        copy = pltpu.make_async_copy(out_ref.at[part], far_ref.at[part], sems.at[n])
        copy.start()
        copies.append(copy)
    for copy in copies:
        copy.wait()


def room(mebibytes):
    return pltpu.CompilerParams(vmem_limit_bytes=mebibytes * 1024 * 1024)


def like(shape, dtype):
    return jax.ShapeDtypeStruct(shape, dtype)


def on_device(
    state,
    kernel,
    w_state,
    w_conv,
    w_adj,
    bias_in,
    w_out,
    obs_op,
    observations,
    obs_mask,
    dual_in,
    dual_res,
    dual_prev,
    dual_bias,
    dual_out_w,
    footprint,
):
    channels, lat_rows, lon_cols = state.shape
    radiance = obs_op.shape[0]
    hid = w_state.shape[0]
    owners = lax.axis_size("band")
    lon_count = lax.axis_size("lon")
    nblocks = lat_rows * lon_cols // PIX
    columns = lat_rows * lon_cols
    side = math.isqrt(owners // 2)
    slots = side * side
    device = [[[(y * side + z) * 2 + c for c in range(2)] for z in range(side)] for y in range(side)]
    by_y = [[[device[y][z][c] for y in range(side)] for z in range(side)] for c in range(2)]
    by_z = [[[device[y][z][c] for z in range(side)] for y in range(side)] for c in range(2)]
    first, second = (by_y[0] + by_z[1], by_z[0] + by_y[1])
    swap = [(i, i ^ 1) for i in range(owners)]
    core = lax.axis_index("band") % 2

    def exchange(value, groups):
        return lax.all_to_all(
            value, "band", split_axis=0, concat_axis=0, axis_index_groups=groups, tiled=True
        )

    routes = footprint.reshape(nblocks * TOP)
    flat = state.reshape(channels, columns)
    projected = jnp.dot(obs_op, flat, preferred_element_type=jnp.float32).astype(jnp.bfloat16)
    rider = jnp.pad(routes.astype(jnp.bfloat16)[None], ((0, 7), (0, columns - nblocks * TOP)))
    projected = jnp.concatenate([projected, rider])
    projected_other = lax.ppermute(projected, "band", swap)
    shares, slot = pl.pallas_call(
        scatter_kernel,
        out_shape=(
            like((slots, radiance, PIX), jnp.bfloat16),
            like((2 * nblocks * TOP,), jnp.int32),
        ),
        in_specs=[SMEM, SMEM, VMEM, VMEM],
        out_specs=(VMEM, SMEM),
        scratch_shapes=[
            pltpu.VMEM((8, PIX), jnp.int32),
            pltpu.SMEM((8, PIX), jnp.int32),
            pltpu.SemaphoreType.DMA,
        ],
        compiler_params=room(8),
        name="scatter",
    )(core.reshape(1), routes, projected, projected_other)
    arrived = exchange(shares, first)

    flat_late, _ = lax.optimization_barrier((flat, slot))
    up = [(i, (i + 1) % lon_count) for i in range(lon_count)]
    down = [(j, i) for i, j in up]
    lanes = [0, lon_cols // PIX, lon_cols // PIX - 1, columns // PIX - 1]
    initial, final = pl.pallas_call(
        edges_kernel,
        out_shape=(like((channels, PIX), jnp.bfloat16),) * 2,
        grid=(1,),
        in_specs=[pl.BlockSpec((channels, PIX), lambda i, n=n: (0, n)) for n in lanes],
        out_specs=(pl.BlockSpec((channels, PIX), lambda i: (0, 0)),) * 2,
        compiler_params=room(4),
        name="edges",
    )(flat_late, flat_late, flat_late, flat_late)
    before = lax.ppermute(final, "lon", up)
    after = lax.ppermute(initial, "lon", down)
    taps = kernel.reshape(channels, 9)
    local, to_up, to_down = pl.pallas_call(
        stencil_kernel,
        out_shape=(
            like((hid, columns), jnp.float32),
            like((hid, lon_cols), jnp.bfloat16),
            like((hid, lon_cols), jnp.bfloat16),
        ),
        in_specs=[VMEM] * 5,
        out_specs=(VMEM,) * 3,
        scratch_shapes=[pltpu.VMEM((channels, 2 * columns), jnp.bfloat16)],
        compiler_params=room(20),
        name="stencil",
    )(flat_late, taps, before, after, w_conv.T)
    arrived, local, to_up, to_down = lax.optimization_barrier((arrived, local, to_up, to_down))

    summed = pl.pallas_call(
        sum_kernel,
        out_shape=like((side, radiance, PIX), jnp.bfloat16),
        in_specs=[HBM],
        out_specs=VMEM,
        scratch_shapes=[
            pltpu.VMEM((side, side, radiance, PIX), jnp.bfloat16),
            pltpu.VMEM((side, radiance, PIX), jnp.float32),
            pltpu.SemaphoreType.DMA((side,)),
        ],
        compiler_params=room(6),
        name="sum",
    )(arrived.reshape(side, side, radiance, PIX))
    summed, to_up, to_down = lax.optimization_barrier((summed, to_up, to_down))
    evolved = jnp.sum(exchange(summed, second), axis=0, dtype=jnp.float32)

    observed = observations.reshape(radiance, PIX)
    valid = obs_mask.reshape(radiance, PIX)
    dual_now = dual_in.reshape(radiance, PIX)
    departure = jnp.where(valid == 1, evolved - observed, 0.0).astype(jnp.bfloat16)
    pre_dual = jnp.dot(dual_res, departure, preferred_element_type=jnp.float32)
    pre_dual = pre_dual + jnp.dot(dual_prev, dual_now, preferred_element_type=jnp.float32)
    dual_hidden = jax.nn.gelu(pre_dual + dual_bias[:, None]).astype(jnp.bfloat16)
    dual_new = (
        dual_now.astype(jnp.float32)
        + jnp.dot(dual_out_w, dual_hidden, preferred_element_type=jnp.float32)
    ).astype(jnp.bfloat16)

    column_of = exchange(jnp.broadcast_to(dual_new, (side, radiance, PIX)), second)
    spread = jnp.broadcast_to(column_of, (side, side, radiance, PIX)).reshape(slots, radiance, PIX)
    spread, flat_last, obs_last = lax.optimization_barrier((spread, flat_late, obs_op))
    all_of = exchange(spread, first)
    onward = [(i, i + 1) for i in range(owners - 1)]
    above = lax.ppermute(to_down, "band", onward)
    below = lax.ppermute(to_up, "band", [(j, i) for i, j in onward])
    local = local + jnp.dot(w_state, flat_last, preferred_element_type=jnp.float32)
    base = local + jnp.concatenate([above, below], axis=1).astype(jnp.float32) + bias_in[:, None]
    lift = across(w_adj, obs_last, ((1,), (1,))).astype(jnp.bfloat16)
    all_of, base, lift = lax.optimization_barrier((all_of, base, lift))
    back_own, back_other = pl.pallas_call(
        gather_kernel,
        out_shape=(
            like((radiance, columns), jnp.float32),
            like((radiance, columns), jnp.bfloat16),
        ),
        in_specs=[SMEM, VMEM],
        out_specs=(VMEM, VMEM),
        compiler_params=room(8),
        name="gather",
    )(slot, all_of)
    back_from = lax.ppermute(back_other, "band", swap)

    state_out = pl.pallas_call(
        update_kernel,
        out_shape=like(state.shape, jnp.bfloat16),
        in_specs=[VMEM] * 6,
        out_specs=HBM,
        scratch_shapes=[
            pltpu.VMEM((hid, columns), jnp.bfloat16),
            pltpu.VMEM(state.shape, jnp.bfloat16),
            pltpu.SemaphoreType.DMA((-(-channels // CHUNK),)),
        ],
        compiler_params=room(16),
        name="update",
    )(base, back_own, back_from, lift, w_out, flat_last)
    return (state_out, dual_new.reshape(radiance, 1, PIX))


def solution(mesh):
    in_specs = (
        P(None, "band", "lon"),
        P(),
        P(),
        P(),
        P(),
        P(),
        P(),
        P(),
        P(None, "band", "lon"),
        P(None, "band", "lon"),
        P(None, "band", "lon"),
        P(),
        P(),
        P(),
        P(),
        P("band", "lon", None, None),
    )
    out_specs = (P(None, "band", "lon"), P(None, "band", "lon"))
    return jax.shard_map(
        on_device, mesh=mesh, in_specs=in_specs, out_specs=out_specs, check_vma=False
    )
```

time: 137 us -> 118 us (0.86)
  Pallas kernels: 25.8 us -> 15.6 us
  starting transfers between devices: 51.3 us -> 46.5 us
  other arithmetic: 3.59 us -> 1.3 us
  local copies, waits for them, and re-layouts: 12.5 us -> 10.7 us
    pallas_call x1, Pallas kernels: 11.5 us -> 5.7 us  [on_device(): pl.pallas_call(stencil_kernel, out_shape=(like((hid, columns), jnp.float3...]
    pallas_call x1, Pallas kernels: 5.54 us -> 2.57 us  [on_device(): pl.pallas_call(update_kernel, out_shape=like(state.shape, jnp.bfloat16),...]
    all_to_all x3, waiting for transfers between devices: 8.76 us -> 11.6 us  [exchange(): lax.all_to_all(value, 'band', split_axis=0, concat_axis=0, axis_index_gro...]
    all_to_all x3, starting transfers between devices: 18.1 us -> 15.7 us  [exchange(): lax.all_to_all(value, 'band', split_axis=0, concat_axis=0, axis_index_gro...]
    reduce_sum x1 -> x0, other arithmetic: 2.4 us -> none  [on_device(): jnp.sum(arrived.reshape(side, side, radiance, PIX), axis=0, dtype=jnp.flo...]
    pad x2 -> x0, local copies, waits for them, and re-layouts: 2.11 us -> none  [the longest x1 1.3 us: on_device(): flat = jnp.pad(state, ((0, extra), (0, 0), (0, 0))).reshape(full, columns)]
    ppermute x1 -> x0, starting transfers between devices: 1.91 us -> none  [on_device(): routes_other = lax.ppermute(routes, 'band', swap)]
    pallas_call x1, Pallas kernels: 4.1 us -> 2.25 us  [on_device(): pl.pallas_call(scatter_kernel, out_shape=(like((slots, radiance, PIX), jn...]
  transfers between devices with their start and end apart: 10 -> 9, of which waited for: 8 -> 9; matrix products, arithmetic and copies ran while one was open for 5% -> 4% of each run, Pallas kernels for 10% -> 6%
where the time goes in v3:
time: 118 us
  starting transfers between devices  46.5 us (39%)
  waiting for transfers between devices  29.6 us (25%)
  Pallas kernels  15.6 us (13%)
  blocking collectives  11 us (9%)
  local copies, waits for them, and re-layouts  10.7 us (9%)
  matrix products  2.08 us (2%)
  other arithmetic  1.3 us (1%)
    all_to_all x3, starting transfers between devices, exchange(): lax.all_to_all(value, 'band', split_axis=0, concat_axis=0, axis_index_gro...  15.7 us
    all_to_all x3, waiting for transfers between devices, exchange(): lax.all_to_all(value, 'band', split_axis=0, concat_axis=0, axis_index_gro...  11.6 us
    all_to_all x1, blocking collectives, exchange(): lax.all_to_all(value, 'band', split_axis=0, concat_axis=0, axis_index_gro...  11 us
    ppermute x1, waiting for transfers between devices, on_device(): above = lax.ppermute(to_down, 'band', onward)  10.6 us
    ppermute x1, starting transfers between devices, on_device(): projected_other = lax.ppermute(projected, 'band', swap)  8.75 us
    ppermute x1, starting transfers between devices, on_device(): back_from = lax.ppermute(back_other, 'band', swap)  7.24 us
    unnamed x49, local copies, waits for them, and re-layouts  7.21 us
    ppermute x1, starting transfers between devices, on_device(): above = lax.ppermute(to_down, 'band', onward)  6.42 us
  transfers between devices with their start and end apart: 9, of which 9 were waited for; matrix products, arithmetic and copies ran while one was open for 4% of the time, Pallas kernels for 6%

profile of v3, /device:TPU:1, one launch (start us, length us, event | category | flops | bytes accessed | tf_op | source)
XLA Modules:
  0.0 117.7 jit_solution(8556345688871189524)
XLA Ops:
  0.6 0.0 copy-start
  0.6 2.8 %pad.10 = bf16[824,2,512]{2,1,0:T(2,128)(2,1)S(1)} pad(bf16[822,2,512]{2,1,0:T(2,128)(2,1)} %param.16, bf16[]{:T(256)} %constant.27.clone.1), padding=0_2x0_0x0_0 | pad | bytes 3371010
  3.4 0.0 copy-start.17
  3.5 0.0 copy-start.10
  3.5 0.4 copy.39
  3.9 0.2 copy-done.17
  4.1 0.1 copy.31
  4.2 0.1 convert_element_type.45
  4.3 0.1 copy-done.10
  4.4 0.5 convolution_convert_fusion
  4.9 8.7 %collective-permute-start = (bf16[104,1024]{1,0:T(8,128)(2,1)S(1)}, bf16[104,1024]{1,0:T(8,128)(2,1)S(1)}, u32[]{:S(2)}, u32[]{:S(2)}) collective-permute-start(bf16[104,1024]{1,0:T(8,128)(2,1)S(1)} %fusion.5.own_ref), channel_id=1, source_target_pairs={{0,4},{4,0},{8,12},{12,8},{16,20},{20,16},{24,28},{28,24},{32,36},... | collective-permute-start | bytes 638984 | tf_op jit(solution)/shard_map/ppermute | solution.py:236
  13.7 0.1 copy.30
  13.8 0.1 reshape.49.own_route_ref
  13.9 0.9 collective-permute-done.other_ref
  14.8 2.2 %scatter.1 = (bf16[64,96,128]{2,1,0:T(8,128)(2,1)S(1)}, s32[64]{0:T(128)S(1)}) custom-call(s32[1]{0:T(128)} %bitcast.1.core_ref, s32[32]{0:T(128)S(1)} %reshape.49.own_route_ref, bf16[104,1024]{1,0:T(8,128)(2,1)S(1)} %fusion.5.own_ref, bf16[104,1024]{1,0:T(8,128)(2,1)S(1)} %collective-permute-done.other_ref), custom_call_target="tpu_custom_call" | custom-call | tf_op jit(solution)/shard_map/scatter/pallas_call | solution.py:237
  17.0 0.0 copy-start.1
  17.0 1.1 copy-done.1
  18.2 4.7 %all-to-all-start = ((bf16[64,96,128]{2,1,0:T(8,128)(2,1)}), bf16[64,96,128]{2,1,0:T(8,128)(2,1)}, u32[]{:S(2)}, u32[]{:S(2)}) async-start(bf16[64,96,128]{2,1,0:T(8,128)(2,1)} %copy-done.1), calls=%async_computation | async-start | bytes 3145728 | tf_op jit(solution)/shard_map/all_to_all | solution.py:227
  22.9 0.0 copy-start.4
  22.9 1.0 edges.1
  23.9 3.1 %collective-permute-start.1 = (bf16[822,128]{1,0:T(8,128)(2,1)}, bf16[822,128]{1,0:T(8,128)(2,1)S(1)}, u32[]{:S(2)}, u32[]{:S(2)}) collective-permute-start(bf16[822,128]{1,0:T(8,128)(2,1)} %get-tuple-element.28), channel_id=1, source_target_pairs={{0,1},{1,2},{2,3},{3,0},{4,5},{5,6},{6,7},{7,4},{8,9},{9,10},{10,1... | collective-permute-start | bytes 631304 | tf_op jit(solution)/shard_map/ppermute | solution.py:268
  27.0 3.4 %collective-permute-start.2 = (bf16[822,128]{1,0:T(8,128)(2,1)}, bf16[822,128]{1,0:T(8,128)(2,1)S(1)}, u32[]{:S(2)}, u32[]{:S(2)}) collective-permute-start(bf16[822,128]{1,0:T(8,128)(2,1)} %get-tuple-element.29), channel_id=1, source_target_pairs={{1,0},{2,1},{3,2},{0,3},{5,4},{6,5},{7,6},{4,7},{9,8},{10,9},{11,1... | collective-permute-start | bytes 631304 | tf_op jit(solution)/shard_map/ppermute | solution.py:269
  30.4 0.0 copy-done.14
  30.4 0.6 reshape.51
  31.0 1.0 copy.32.taps_ref
  32.0 2.0 %collective-permute-done.1.before_ref = bf16[822,128]{1,0:T(8,128)(2,1)S(1)} collective-permute-done((bf16[822,128]{1,0:T(8,128)(2,1)}, bf16[822,128]{1,0:T(8,128)(2,1)S(1)}, u32[]{:S(2)}, u32[]{:S(2)}) %collective-permute-start.1) | collective-permute-done | bytes 210464 | tf_op jit(solution)/shard_map/ppermute | solution.py:268
  34.1 1.6 %collective-permute-done.2.after_ref = bf16[822,128]{1,0:T(8,128)(2,1)S(1)} collective-permute-done((bf16[822,128]{1,0:T(8,128)(2,1)}, bf16[822,128]{1,0:T(8,128)(2,1)S(1)}, u32[]{:S(2)}, u32[]{:S(2)}) %collective-permute-start.2) | collective-permute-done | bytes 210464 | tf_op jit(solution)/shard_map/ppermute | solution.py:269
  35.7 0.0 copy-done.4
  35.7 5.7 %stencil.1 = (f32[256,1024]{1,0:T(8,128)S(1)}, bf16[256,512]{1,0:T(8,128)(2,1)S(1)}, bf16[256,512]{1,0:T(8,128)(2,1)S(1)}) custom-call(bf16[822,1024]{1,0:T(8,128)(2,1)S(1)} %bitcast.58, f32[822,9]{1,0:T(8,128)S(1)} %copy.32.taps_ref, bf16[822,128]{1,0:T(8,128)(2,1)S(1)} %collective-permute-done.1.before_ref, ...), custom_call_target="tpu_custom_call" | custom-call | tf_op jit(solution)/shard_map/stencil/pallas_call | solution.py:271
  41.4 0.0 copy-start.2
  41.4 1.0 copy-done.2
  42.4 0.7 copy-done.6
  43.1 0.7 copy-done.8
  43.8 0.0 copy-start.20
  43.8 0.0 copy-start.21
  43.8 0.0 copy-start.22
  43.8 2.9 %all-to-all-done = bf16[64,96,128]{2,1,0:T(8,128)(2,1)} async-done(((bf16[64,96,128]{2,1,0:T(8,128)(2,1)}), bf16[64,96,128]{2,1,0:T(8,128)(2,1)}, u32[]{:S(2)}, u32[]{:S(2)}) %all-to-all-start) | async-done | bytes 1572896 | tf_op jit(solution)/shard_map/all_to_all | solution.py:227
  46.7 2.3 %sum.1 = bf16[8,96,128]{2,1,0:T(8,128)(2,1)} custom-call(bf16[8,8,96,128]{3,2,1,0:T(8,128)(2,1)} %bitcast.3.far_ref), custom_call_target="tpu_custom_call" | custom-call | tf_op jit(solution)/shard_map/sum/pallas_call | solution.py:286
  48.9 6.5 %all-to-all-start.1 = ((bf16[8,96,128]{2,1,0:T(8,128)(2,1)}), bf16[8,96,128]{2,1,0:T(8,128)(2,1)S(1)}, u32[]{:S(2)}, u32[]{:S(2)}) async-start(bf16[8,96,128]{2,1,0:T(8,128)(2,1)} %sum.1), calls=%async_computation.1 | async-start | bytes 393216 | tf_op jit(solution)/shard_map/all_to_all | solution.py:227
  55.5 0.0 copy-done.12
  55.5 0.1 broadcast_compare_fusion
  55.6 0.0 copy-done.13
  55.6 0.2 fusion.19
  55.8 8.3 %all-to-all-done.1 = bf16[8,96,128]{2,1,0:T(8,128)(2,1)S(1)} async-done(((bf16[8,96,128]{2,1,0:T(8,128)(2,1)}), bf16[8,96,128]{2,1,0:T(8,128)(2,1)S(1)}, u32[]{:S(2)}, u32[]{:S(2)}) %all-to-all-start.1) | async-done | bytes 196640 | tf_op jit(solution)/shard_map/all_to_all | solution.py:227
  64.2 0.4 fusion.3
  64.6 0.0 copy-start.16
  64.6 11.0 %all_to_all.20 = bf16[8,96,128]{2,1,0:T(8,128)(2,1)S(1)} all-to-all(bf16[8,96,128]{2,1,0:T(8,128)(2,1)S(1)} %broadcast_in_dim.14), channel_id=1, replica_groups={{0,8,16,24,32,40,48,56},{64,72,80,88,96,104,112,120},{128,136,144,152,1..., dimensions={0} | all-to-all | bytes 393216 | tf_op jit(solution)/shard_map/all_to_all | solution.py:227
  75.6 1.4 %broadcast_in_dim.15 = bf16[8,8,96,128]{3,2,1,0:T(8,128)(2,1)} broadcast(bf16[8,96,128]{2,1,0:T(8,128)(2,1)S(1)} %all_to_all.20), dimensions={1,2,3} | broadcast | bytes 1769472 | tf_op jit(solution)/shard_map/broadcast_in_dim | solution.py:315
  77.0 4.4 %all-to-all-start.3 = ((bf16[64,96,128]{2,1,0:T(8,128)(2,1)}), bf16[64,96,128]{2,1,0:T(8,128)(2,1)}, u32[]{:S(2)}, u32[]{:S(2)}) async-start(bf16[64,96,128]{2,1,0:T(8,128)(2,1)} %bitcast.64), calls=%async_computation.3 | async-start | bytes 3145728 | tf_op jit(solution)/shard_map/all_to_all | solution.py:227
  81.5 6.4 %collective-permute-start.3 = (bf16[256,512]{1,0:T(8,128)(2,1)S(1)}, bf16[256,512]{1,0:T(8,128)(2,1)}, u32[]{:S(2)}, u32[]{:S(2)}) collective-permute-start(bf16[256,512]{1,0:T(8,128)(2,1)S(1)} %copy-done.9), channel_id=1, source_target_pairs={{0,4},{4,8},{8,12},{12,16},{16,20},{20,24},{24,28},{28,32},{32,36}... | collective-permute-start | bytes 786440 | tf_op jit(solution)/shard_map/ppermute | solution.py:319
  87.9 1.9 %collective-permute-start.4 = (bf16[256,512]{1,0:T(8,128)(2,1)S(1)}, bf16[256,512]{1,0:T(8,128)(2,1)}, u32[]{:S(2)}, u32[]{:S(2)}) collective-permute-start(bf16[256,512]{1,0:T(8,128)(2,1)S(1)} %copy-done.7), channel_id=1, source_target_pairs={{4,0},{8,4},{12,8},{16,12},{20,16},{24,20},{28,24},{32,28},{36,32}... | collective-permute-start | bytes 786440 | tf_op jit(solution)/shard_map/ppermute | solution.py:320
  89.9 0.2 convolution_convert_fusion.1
  90.1 0.1 copy.35
  90.2 0.0 copy-start.18
  90.2 0.8 convolution_bitcast_fusion
  91.0 10.6 %collective-permute-done.3 = bf16[256,512]{1,0:T(8,128)(2,1)} collective-permute-done((bf16[256,512]{1,0:T(8,128)(2,1)S(1)}, bf16[256,512]{1,0:T(8,128)(2,1)}, u32[]{:S(2)}, u32[]{:S(2)}) %collective-permute-start.3) | collective-permute-done | bytes 262176 | tf_op jit(solution)/shard_map/ppermute | solution.py:319
  101.6 1.8 %collective-permute-done.4 = bf16[256,512]{1,0:T(8,128)(2,1)} collective-permute-done((bf16[256,512]{1,0:T(8,128)(2,1)S(1)}, bf16[256,512]{1,0:T(8,128)(2,1)}, u32[]{:S(2)}, u32[]{:S(2)}) %collective-permute-start.4) | collective-permute-done | bytes 262176 | tf_op jit(solution)/shard_map/ppermute | solution.py:320
  103.4 0.0 copy-done.3
  103.4 1.2 %add_add_fusion.base_ref = f32[256,1024]{1,0:T(8,128)S(1)} fusion(f32[256,1024]{1,0:T(8,128)S(1)} %copy-done.3, f32[256,1024]{1,0:T(8,128)S(1)} %convolution_bitcast_fusion, bf16[256,512]{1,0:T(8,128)(2,1)} %collective-permute-done.4, bf16[256,512]{1,0:T(8,128)(2,1)} %collective-permute-done.3, f32[256]{0:T(256)S(1)} %copy-done.18), kind=kLoop, calls=%fused_computation.9 | loop fusion | flops 1835008 | bytes 3671040 | tf_op jit(solution)/shard_map/add | solution.py:322
  104.6 0.4 all-to-all-done.3.dual_ref
  105.0 1.8 %gather.1 = (f32[96,1024]{1,0:T(8,128)S(1)}, bf16[96,1024]{1,0:T(8,128)(2,1)S(1)}) custom-call(s32[64]{0:T(128)S(1)} %get-tuple-element.26.slot_ref, bf16[64,96,128]{2,1,0:T(8,128)(2,1)} %all-to-all-done.3.dual_ref), custom_call_target="tpu_custom_call" | custom-call | tf_op jit(solution)/shard_map/gather/pallas_call | solution.py:325
  106.8 7.2 %collective-permute-start.5 = (bf16[96,1024]{1,0:T(8,128)(2,1)S(1)}, bf16[96,1024]{1,0:T(8,128)(2,1)S(1)}, u32[]{:S(2)}, u32[]{:S(2)}) collective-permute-start(bf16[96,1024]{1,0:T(8,128)(2,1)S(1)} %get-tuple-element.46), channel_id=1, source_target_pairs={{0,4},{4,0},{8,12},{12,8},{16,20},{20,16},{24,28},{28,24},{32,36},... | collective-permute-start | bytes 589832 | tf_op jit(solution)/shard_map/ppermute | solution.py:336
  114.1 1.0 collective-permute-done.5.other_ref
  115.1 2.6 %update.1 = bf16[822,2,512]{2,1,0:T(2,128)(2,1)} custom-call(f32[256,1024]{1,0:T(8,128)S(1)} %add_add_fusion.base_ref, f32[96,1024]{1,0:T(8,128)S(1)} %get-tuple-element.45.own_ref, bf16[96,1024]{1,0:T(8,128)(2,1)S(1)} %collective-permute-done.5.other_ref, bf16[256,96]{1,0:T(8,128)(2,1)S(1)} %bitcast.62, bf16[822,256]{1,0:T(8,128)(2,1)S(1)} %copy-done.5, ...), custom_call_target="tpu_custom_call" | custom-call | tf_op jit(solution)/shard_map/update/pallas_call | solution.py:338
  (28 shorter events, 0.1 us)
Async XLA Ops:
  0.6 89.6 %copy-start = (bf16[256,822]{0,1:T(8,128)(2,1)S(1)}, bf16[256,822]{0,1:T(8,128)(2,1)}, u32[]{:S(2)}) copy-start(bf16[256,822]{0,1:T(8,128)(2,1)} %param.18) | copy-start | bytes 1262596
  3.4 0.7 copy-start.17
  3.5 0.9 copy-start.10
  4.9 9.8 %collective-permute-start = (bf16[104,1024]{1,0:T(8,128)(2,1)S(1)}, bf16[104,1024]{1,0:T(8,128)(2,1)S(1)}, u32[]{:S(2)}, u32[]{:S(2)}) collective-permute-start(bf16[104,1024]{1,0:T(8,128)(2,1)S(1)} %fusion.5.own_ref), channel_id=1, source_target_pairs={{0,4},{4,0},{8,12},{12,8},{16,20},{20,16},{24,28},{28,24},{32,36},... | collective-permute-start | bytes 638984 | tf_op jit(solution)/shard_map/ppermute | solution.py:236
  17.0 1.1 copy-start.1
  18.2 28.5 %all-to-all-start = ((bf16[64,96,128]{2,1,0:T(8,128)(2,1)}), bf16[64,96,128]{2,1,0:T(8,128)(2,1)}, u32[]{:S(2)}, u32[]{:S(2)}) async-start(bf16[64,96,128]{2,1,0:T(8,128)(2,1)} %copy-done.1), calls=%async_computation | async-start | bytes 3145728 | tf_op jit(solution)/shard_map/all_to_all | solution.py:227
  22.8 7.5 %copy-start.14 = (f32[822,3,3]{0,2,1:T(4,128)S(1)}, f32[822,3,3]{0,2,1:T(4,128)}, u32[]{:S(2)}) copy-start(f32[822,3,3]{0,2,1:T(4,128)} %param.17) | copy-start | bytes 88780
  22.9 12.8 %copy-start.4 = (bf16[256,822]{0,1:T(8,128)(2,1)S(1)}, bf16[256,822]{0,1:T(8,128)(2,1)}, u32[]{:S(2)}) copy-start(bf16[256,822]{0,1:T(8,128)(2,1)} %param.19) | copy-start | bytes 1262596
  23.9 10.2 %collective-permute-start.1 = (bf16[822,128]{1,0:T(8,128)(2,1)}, bf16[822,128]{1,0:T(8,128)(2,1)S(1)}, u32[]{:S(2)}, u32[]{:S(2)}) collective-permute-start(bf16[822,128]{1,0:T(8,128)(2,1)} %get-tuple-element.28), channel_id=1, source_target_pairs={{0,1},{1,2},{2,3},{3,0},{4,5},{5,6},{6,7},{7,4},{8,9},{9,10},{10,1... | collective-permute-start | bytes 631304 | tf_op jit(solution)/shard_map/ppermute | solution.py:268
  27.0 8.7 %collective-permute-start.2 = (bf16[822,128]{1,0:T(8,128)(2,1)}, bf16[822,128]{1,0:T(8,128)(2,1)S(1)}, u32[]{:S(2)}, u32[]{:S(2)}) collective-permute-start(bf16[822,128]{1,0:T(8,128)(2,1)} %get-tuple-element.29), channel_id=1, source_target_pairs={{1,0},{2,1},{3,2},{0,3},{5,4},{6,5},{7,6},{4,7},{9,8},{10,9},{11,1... | collective-permute-start | bytes 631304 | tf_op jit(solution)/shard_map/ppermute | solution.py:269
  41.4 1.0 copy-start.2
  42.4 0.7 copy-start.6
  43.1 0.7 copy-start.8
  43.8 11.7 %copy-start.12 = (s32[96,1,128]{2,1,0:T(1,128)S(1)}, s32[96,1,128]{2,1,0:T(1,128)}, u32[]{:S(2)}) copy-start(s32[96,1,128]{2,1,0:T(1,128)} %param.25) | copy-start | bytes 147460
  43.8 11.8 %copy-start.13 = (bf16[256,96]{0,1:T(8,128)(2,1)S(1)}, bf16[256,96]{0,1:T(8,128)(2,1)}, u32[]{:S(2)}) copy-start(bf16[256,96]{0,1:T(8,128)(2,1)} %param.28) | copy-start | bytes 147460
  43.8 11.8 %copy-start.15 = (bf16[96,1,128]{2,0,1:T(8,128)(2,1)S(1)}, bf16[96,1,128]{2,0,1:T(8,128)(2,1)}, u32[]{:S(2)}) copy-start(bf16[96,1,128]{2,0,1:T(8,128)(2,1)} %param.26) | copy-start | bytes 73732
  43.8 20.4 %copy-start.19 = (bf16[96,256]{1,0:T(8,128)(2,1)S(1)}, bf16[96,256]{1,0:T(8,128)(2,1)}, u32[]{:S(2)}) copy-start(bf16[96,256]{1,0:T(8,128)(2,1)} %param.30) | copy-start | bytes 147460
  43.8 20.4 %copy-start.20 = (bf16[256,96]{0,1:T(8,128)(2,1)S(1)}, bf16[256,96]{0,1:T(8,128)(2,1)}, u32[]{:S(2)}) copy-start(bf16[256,96]{0,1:T(8,128)(2,1)} %param.27) | copy-start | bytes 147460
  43.8 20.4 %copy-start.21 = (f32[96,1,128]{2,1,0:T(1,128)S(1)}, f32[96,1,128]{2,1,0:T(1,128)}, u32[]{:S(2)}) copy-start(f32[96,1,128]{2,1,0:T(1,128)} %param.24) | copy-start | bytes 147460
  43.8 20.4 %copy-start.22 = (f32[256]{0:T(256)S(1)}, f32[256]{0:T(256)}, u32[]{:S(2)}) copy-start(f32[256]{0:T(256)} %param.29) | copy-start | bytes 3076
  48.9 15.2 %all-to-all-start.1 = ((bf16[8,96,128]{2,1,0:T(8,128)(2,1)}), bf16[8,96,128]{2,1,0:T(8,128)(2,1)S(1)}, u32[]{:S(2)}, u32[]{:S(2)}) async-start(bf16[8,96,128]{2,1,0:T(8,128)(2,1)} %sum.1), calls=%async_computation.1 | async-start | bytes 393216 | tf_op jit(solution)/shard_map/all_to_all | solution.py:227
  64.6 12.5 %copy-start.16 = (bf16[96,128]{1,0:T(8,128)(2,1)}, bf16[96,128]{1,0:T(8,128)(2,1)S(1)}, u32[]{:S(2)}) copy-start(bf16[96,128]{1,0:T(8,128)(2,1)S(1)} %fusion.3) | copy-start | bytes 73732
  77.0 4.5 %copy-start.9 = (bf16[256,512]{1,0:T(8,128)(2,1)S(1)}, bf16[256,512]{1,0:T(8,128)(2,1)}, u32[]{:S(2)}) copy-start(bf16[256,512]{1,0:T(8,128)(2,1)} %copy-done.8) | copy-start | bytes 786436
  77.0 10.9 %copy-start.7 = (bf16[256,512]{1,0:T(8,128)(2,1)S(1)}, bf16[256,512]{1,0:T(8,128)(2,1)}, u32[]{:S(2)}) copy-start(bf16[256,512]{1,0:T(8,128)(2,1)} %copy-done.6) | copy-start | bytes 786436
  77.0 12.8 %copy-start.11 = (bf16[256,822]{0,1:T(8,128)(2,1)S(1)}, bf16[256,822]{0,1:T(8,128)(2,1)}, u32[]{:S(2)}) copy-start(bf16[256,822]{0,1:T(8,128)(2,1)} %param.20) | copy-start | bytes 1262596
  77.0 28.0 %all-to-all-start.3 = ((bf16[64,96,128]{2,1,0:T(8,128)(2,1)}), bf16[64,96,128]{2,1,0:T(8,128)(2,1)}, u32[]{:S(2)}, u32[]{:S(2)}) async-start(bf16[64,96,128]{2,1,0:T(8,128)(2,1)} %bitcast.64), calls=%async_computation.3 | async-start | bytes 3145728 | tf_op jit(solution)/shard_map/all_to_all | solution.py:227
  81.5 20.1 %collective-permute-start.3 = (bf16[256,512]{1,0:T(8,128)(2,1)S(1)}, bf16[256,512]{1,0:T(8,128)(2,1)}, u32[]{:S(2)}, u32[]{:S(2)}) collective-permute-start(bf16[256,512]{1,0:T(8,128)(2,1)S(1)} %copy-done.9), channel_id=1, source_target_pairs={{0,4},{4,8},{8,12},{12,16},{16,20},{20,24},{24,28},{28,32},{32,36}... | collective-permute-start | bytes 786440 | tf_op jit(solution)/shard_map/ppermute | solution.py:319
  87.9 15.5 %collective-permute-start.4 = (bf16[256,512]{1,0:T(8,128)(2,1)S(1)}, bf16[256,512]{1,0:T(8,128)(2,1)}, u32[]{:S(2)}, u32[]{:S(2)}) collective-permute-start(bf16[256,512]{1,0:T(8,128)(2,1)S(1)} %copy-done.7), channel_id=1, source_target_pairs={{4,0},{8,4},{12,8},{16,12},{20,16},{24,20},{28,24},{32,28},{36,32}... | collective-permute-start | bytes 786440 | tf_op jit(solution)/shard_map/ppermute | solution.py:320
  90.2 13.2 %copy-start.3 = (f32[256,1024]{1,0:T(8,128)S(1)}, f32[256,1024]{1,0:T(8,128)}, u32[]{:S(2)}) copy-start(f32[256,1024]{1,0:T(8,128)} %copy-done.2) | copy-start | bytes 3145732
  90.2 13.2 %copy-start.18 = (f32[256]{0:T(256)S(1)}, f32[256]{0:T(256)}, u32[]{:S(2)}) copy-start(f32[256]{0:T(256)} %param.21) | copy-start | bytes 3076
  105.0 10.1 %copy-start.5 = (bf16[822,256]{1,0:T(8,128)(2,1)S(1)}, bf16[822,256]{1,0:T(8,128)(2,1)}, u32[]{:S(2)}) copy-start(bf16[822,256]{1,0:T(8,128)(2,1)} %wo_ref.1) | copy-start | bytes 1262596
  106.8 8.3 %collective-permute-start.5 = (bf16[96,1024]{1,0:T(8,128)(2,1)S(1)}, bf16[96,1024]{1,0:T(8,128)(2,1)S(1)}, u32[]{:S(2)}, u32[]{:S(2)}) collective-permute-start(bf16[96,1024]{1,0:T(8,128)(2,1)S(1)} %get-tuple-element.46), channel_id=1, source_target_pairs={{0,4},{4,0},{8,12},{12,8},{16,20},{20,16},{24,28},{28,24},{32,36},... | collective-permute-start | bytes 589832 | tf_op jit(solution)/shard_map/ppermute | solution.py:336

commit v4 on v3

--- a/solution.py
+++ b/solution.py
@@ -19,6 +19,16 @@
 
 def across(a, b, dims):
     return lax.dot_general(a, b, (dims, ((), ())), preferred_element_type=jnp.float32)
+
+
+def fetch_kernel(state_ref, out_ref, sem):
+    rows = state_ref.shape[0]
+    copy = pltpu.make_async_copy(state_ref, out_ref.at[pl.ds(0, rows)], sem)
+    copy.start()
+    spare = (out_ref.shape[0] - rows,) + tuple(out_ref.shape[1:])
+    if spare[0] > 0:
+        out_ref[rows:] = jnp.zeros(spare, out_ref.dtype)
+    copy.wait()
 
 
 def edges_kernel(first0_ref, first1_ref, last0_ref, last1_ref, first_ref, last_ref):
@@ -88,28 +98,10 @@
             ref[:, k * PIX : (k + 1) * PIX] = total.astype(ref.dtype)
 
 
-def sum_kernel(far_ref, out_ref, part_ref, total_ref, sems):
-    count = far_ref.shape[0]
-    copies = [pltpu.make_async_copy(far_ref.at[i], part_ref.at[i], sems.at[i]) for i in range(count)]
-    for copy in copies:
-        copy.start()
-    for i in range(0, count, 2):
-        copies[i].wait()
-        copies[i + 1].wait()
-        for j in range(out_ref.shape[0]):
-            pair = part_ref[i, j].astype(jnp.float32) + part_ref[i + 1, j].astype(jnp.float32)
-            if i > 0:
-                pair = total_ref[j] + pair
-            if i + 2 < count:
-                total_ref[j] = pair
-            else:
-                out_ref[j] = pair.astype(out_ref.dtype)
-
-
 def stencil_kernel(
     flat_ref, taps_ref, before_ref, after_ref, wc_ref, local_ref, up_ref, down_ref, mixed_ref
 ):
-    channels, columns = flat_ref.shape
+    channels, columns = (wc_ref.shape[0], flat_ref.shape[1])
     half = columns // 2
 
     def piece(rows, count):
@@ -152,16 +144,16 @@
     lax.fori_loop(0, steps, step, 0, unroll=3)
     if channels > steps * SUB:
         piece(slice(steps * SUB, channels), channels - steps * SUB)
-    sent = across(wc_ref[...], mixed_ref[:, columns:], ((0,), (0,))).astype(jnp.bfloat16)
+    sent = across(wc_ref[...], mixed_ref[:channels, columns:], ((0,), (0,))).astype(jnp.bfloat16)
     up_ref[...] = sent[:, :half]
     down_ref[...] = sent[:, half:]
-    local_ref[...] = across(wc_ref[...], mixed_ref[:, :columns], ((0,), (0,)))
+    local_ref[...] = across(wc_ref[...], mixed_ref[:channels, :columns], ((0,), (0,)))
 
 
 def update_kernel(
     base_ref, own_ref, other_ref, lift_ref, wo_ref, flat_ref, far_ref, hidden_ref, out_ref, sems
 ):
-    channels, columns = flat_ref.shape
+    channels, columns = (far_ref.shape[0], flat_ref.shape[1])
     half = columns // 2
     back = (own_ref[...] + other_ref[...].astype(jnp.float32)).astype(jnp.bfloat16)
     pre = base_ref[...] + across(lift_ref[...], back, ((1,), (0,)))
@@ -229,8 +221,18 @@
         )
 
     routes = footprint.reshape(nblocks * TOP)
-    flat = state.reshape(channels, columns)
-    projected = jnp.dot(obs_op, flat, preferred_element_type=jnp.float32).astype(jnp.bfloat16)
+    tall = -(-channels // 8) * 8
+    flat = pl.pallas_call(
+        fetch_kernel,
+        out_shape=like((tall, lat_rows, lon_cols), jnp.bfloat16),
+        in_specs=[HBM],
+        out_specs=VMEM,
+        scratch_shapes=[pltpu.SemaphoreType.DMA],
+        compiler_params=room(4),
+        name="fetch",
+    )(state).reshape(tall, columns)
+    flat = lax.optimization_barrier(flat)
+    projected = jnp.dot(obs_op, flat[:channels], preferred_element_type=jnp.float32).astype(jnp.bfloat16)
     rider = jnp.pad(routes.astype(jnp.bfloat16)[None], ((0, 7), (0, columns - nblocks * TOP)))
     projected = jnp.concatenate([projected, rider])
     projected_other = lax.ppermute(projected, "band", swap)
@@ -258,10 +260,10 @@
     lanes = [0, lon_cols // PIX, lon_cols // PIX - 1, columns // PIX - 1]
     initial, final = pl.pallas_call(
         edges_kernel,
-        out_shape=(like((channels, PIX), jnp.bfloat16),) * 2,
+        out_shape=(like((tall, PIX), jnp.bfloat16),) * 2,
         grid=(1,),
-        in_specs=[pl.BlockSpec((channels, PIX), lambda i, n=n: (0, n)) for n in lanes],
-        out_specs=(pl.BlockSpec((channels, PIX), lambda i: (0, 0)),) * 2,
+        in_specs=[pl.BlockSpec((tall, PIX), lambda i, n=n: (0, n)) for n in lanes],
+        out_specs=(pl.BlockSpec((tall, PIX), lambda i: (0, 0)),) * 2,
         compiler_params=room(4),
         name="edges",
     )(flat_late, flat_late, flat_late, flat_late)
@@ -277,25 +279,18 @@
         ),
         in_specs=[VMEM] * 5,
         out_specs=(VMEM,) * 3,
-        scratch_shapes=[pltpu.VMEM((channels, 2 * columns), jnp.bfloat16)],
+        scratch_shapes=[pltpu.VMEM((-(-channels // SUB) * SUB, 2 * columns), jnp.bfloat16)],
         compiler_params=room(20),
         name="stencil",
     )(flat_late, taps, before, after, w_conv.T)
-    arrived, local, to_up, to_down = lax.optimization_barrier((arrived, local, to_up, to_down))
-
-    summed = pl.pallas_call(
-        sum_kernel,
-        out_shape=like((side, radiance, PIX), jnp.bfloat16),
-        in_specs=[HBM],
-        out_specs=VMEM,
-        scratch_shapes=[
-            pltpu.VMEM((side, side, radiance, PIX), jnp.bfloat16),
-            pltpu.VMEM((side, radiance, PIX), jnp.float32),
-            pltpu.SemaphoreType.DMA((side,)),
-        ],
-        compiler_params=room(6),
-        name="sum",
-    )(arrived.reshape(side, side, radiance, PIX))
+    lift = across(w_adj, obs_op, ((1,), (1,))).astype(jnp.bfloat16)
+    arrived, local, to_up, to_down, lift = lax.optimization_barrier(
+        (arrived, local, to_up, to_down, lift)
+    )
+
+    summed = jnp.sum(
+        arrived.reshape(side, side, radiance, PIX), axis=0, dtype=jnp.float32
+    ).astype(jnp.bfloat16)
     summed, to_up, to_down = lax.optimization_barrier((summed, to_up, to_down))
     evolved = jnp.sum(exchange(summed, second), axis=0, dtype=jnp.float32)
 
@@ -313,15 +308,14 @@
 
     column_of = exchange(jnp.broadcast_to(dual_new, (side, radiance, PIX)), second)
     spread = jnp.broadcast_to(column_of, (side, side, radiance, PIX)).reshape(slots, radiance, PIX)
-    spread, flat_last, obs_last = lax.optimization_barrier((spread, flat_late, obs_op))
+    spread, flat_last = lax.optimization_barrier((spread, flat_late))
     all_of = exchange(spread, first)
     onward = [(i, i + 1) for i in range(owners - 1)]
     above = lax.ppermute(to_down, "band", onward)
     below = lax.ppermute(to_up, "band", [(j, i) for i, j in onward])
-    local = local + jnp.dot(w_state, flat_last, preferred_element_type=jnp.float32)
+    local = local + jnp.dot(w_state, flat_last[:channels], preferred_element_type=jnp.float32)
     base = local + jnp.concatenate([above, below], axis=1).astype(jnp.float32) + bias_in[:, None]
-    lift = across(w_adj, obs_last, ((1,), (1,))).astype(jnp.bfloat16)
-    all_of, base, lift = lax.optimization_barrier((all_of, base, lift))
+    all_of, base = lax.optimization_barrier((all_of, base))
     back_own, back_other = pl.pallas_call(
         gather_kernel,
         out_shape=(

time: 118 us -> 117 us (level)
  waiting for transfers between devices: 29.6 us -> 34.1 us
  local copies, waits for them, and re-layouts: 10.7 us -> 6.39 us
  Pallas kernels: 15.6 us -> 12.8 us
  other arithmetic: 1.3 us -> 2.59 us
    all_to_all x3, waiting for transfers between devices: 11.6 us -> 14.8 us  [exchange(): lax.all_to_all(value, 'band', split_axis=0, concat_axis=0, axis_index_gro...]
    unnamed x49 -> x42, local copies, waits for them, and re-layouts: 7.21 us -> 4.49 us
    pallas_call x2, Pallas kernels: 3.26 us -> 0.55 us  [the longest x1 0.29 us: on_device(): pl.pallas_call(edges_kernel, out_shape=(like((tall, PIX), jnp.bfloat16),)...]
    reduce_sum x0 -> x1, other arithmetic: none -> 2.35 us  [on_device(): jnp.sum(arrived.reshape(side, side, radiance, PIX), axis=0, dtype=jnp.flo...]
    reshape x2, local copies, waits for them, and re-layouts: 1.63 us -> 0.21 us  [on_device(): taps = kernel.reshape(channels, 9)]
  transfers between devices with their start and end apart: 9 -> 9, of which waited for: 9 -> 9; matrix products, arithmetic and copies ran while one was open for 4% -> 2% of each run, Pallas kernels for 6% -> 5%
where the time goes in v4:
time: 117 us
  starting transfers between devices  46.4 us (40%)
  waiting for transfers between devices  34.1 us (29%)
  Pallas kernels  12.8 us (11%)
  blocking collectives  11 us (9%)
  local copies, waits for them, and re-layouts  6.39 us (5%)
  other arithmetic  2.59 us (2%)
  matrix products  2.2 us (2%)
    all_to_all x3, starting transfers between devices, exchange(): lax.all_to_all(value, 'band', split_axis=0, concat_axis=0, axis_index_gro...  15.5 us
    all_to_all x3, waiting for transfers between devices, exchange(): lax.all_to_all(value, 'band', split_axis=0, concat_axis=0, axis_index_gro...  14.8 us
    all_to_all x1, blocking collectives, exchange(): lax.all_to_all(value, 'band', split_axis=0, concat_axis=0, axis_index_gro...  11 us
    ppermute x1, waiting for transfers between devices, on_device(): above = lax.ppermute(to_down, 'band', onward)  10.9 us
    ppermute x1, starting transfers between devices, on_device(): projected_other = lax.ppermute(projected, 'band', swap)  8.75 us
    ppermute x1, starting transfers between devices, on_device(): back_from = lax.ppermute(back_other, 'band', swap)  7.22 us
    ppermute x1, starting transfers between devices, on_device(): above = lax.ppermute(to_down, 'band', onward)  6.53 us
    pallas_call x1, Pallas kernels, on_device(): pl.pallas_call(stencil_kernel, out_shape=(like((hid, columns), jnp.float3...  5.67 us
  transfers between devices with their start and end apart: 9, of which 9 were waited for; matrix products, arithmetic and copies ran while one was open for 2% of the time, Pallas kernels for 5%

profile of v4, /device:TPU:1, one launch (start us, length us, event | category | flops | bytes accessed | tf_op | source)
XLA Modules:
  0.0 116.6 jit_solution(17629540746363308017)
XLA Ops:
  0.6 0.0 copy-start
  0.6 0.0 copy-start.1
  0.7 1.5 %copy-done.1 = bf16[822,2,512]{2,1,0:T(2,128)(2,1)S(1)} copy-done((bf16[822,2,512]{2,1,0:T(2,128)(2,1)S(1)}, bf16[822,2,512]{2,1,0:T(2,128)(2,1)}, u32[]{:S(2)}) %copy-start.1) | copy-done | bytes 1683480
  2.1 0.3 fetch.1
  2.4 0.0 copy-start.13
  2.4 0.0 copy-start.8
  2.4 0.4 copy.40
  2.9 0.2 copy-done.13
  3.1 0.1 copy.32
  3.2 0.1 convert_element_type.44
  3.3 0.1 copy-done.8
  3.3 0.5 fusion.7
  3.9 8.7 %collective-permute-start = (bf16[104,1024]{1,0:T(8,128)(2,1)S(1)}, bf16[104,1024]{1,0:T(8,128)(2,1)S(1)}, u32[]{:S(2)}, u32[]{:S(2)}) collective-permute-start(bf16[104,1024]{1,0:T(8,128)(2,1)S(1)} %fusion.15.own_ref), channel_id=1, source_target_pairs={{0,4},{4,0},{8,12},{12,8},{16,20},{20,16},{24,28},{28,24},{32,36},... | collective-permute-start | bytes 638984 | tf_op jit(solution)/shard_map/ppermute | solution.py:238
  12.7 0.1 copy.31
  12.7 0.1 reshape.49.own_route_ref
  12.8 0.9 collective-permute-done.other_ref
  13.7 2.3 %scatter.1 = (bf16[64,96,128]{2,1,0:T(8,128)(2,1)S(1)}, s32[64]{0:T(128)S(1)}) custom-call(s32[1]{0:T(128)} %bitcast.3.core_ref, s32[32]{0:T(128)S(1)} %reshape.49.own_route_ref, bf16[104,1024]{1,0:T(8,128)(2,1)S(1)} %fusion.15.own_ref, bf16[104,1024]{1,0:T(8,128)(2,1)S(1)} %collective-permute-done.other_ref), custom_call_target="tpu_custom_call" | custom-call | tf_op jit(solution)/shard_map/scatter/pallas_call | solution.py:239
  16.0 0.0 copy-start.2
  16.0 1.1 copy-done.2
  17.1 4.7 %all-to-all-start = ((bf16[64,96,128]{2,1,0:T(8,128)(2,1)}), bf16[64,96,128]{2,1,0:T(8,128)(2,1)}, u32[]{:S(2)}, u32[]{:S(2)}) async-start(bf16[64,96,128]{2,1,0:T(8,128)(2,1)} %copy-done.2), calls=%async_computation | async-start | bytes 3145728 | tf_op jit(solution)/shard_map/all_to_all | solution.py:219
  21.8 0.0 copy-done.10
  21.9 0.2 copy.33.taps_ref
  22.1 0.0 copy-start.7
  22.1 0.0 copy-start.5
  22.1 0.3 edges.1
  22.4 3.1 %collective-permute-start.1 = (bf16[824,128]{1,0:T(8,128)(2,1)S(1)}, bf16[824,128]{1,0:T(8,128)(2,1)S(1)}, u32[]{:S(2)}, u32[]{:S(2)}) collective-permute-start(bf16[824,128]{1,0:T(8,128)(2,1)S(1)} %get-tuple-element.27), channel_id=1, source_target_pairs={{0,1},{1,2},{2,3},{3,0},{4,5},{5,6},{6,7},{7,4},{8,9},{9,10},{10,1... | collective-permute-start | bytes 632840 | tf_op jit(solution)/shard_map/ppermute | solution.py:270
  25.5 3.4 %collective-permute-start.2 = (bf16[824,128]{1,0:T(8,128)(2,1)S(1)}, bf16[824,128]{1,0:T(8,128)(2,1)S(1)}, u32[]{:S(2)}, u32[]{:S(2)}) collective-permute-start(bf16[824,128]{1,0:T(8,128)(2,1)S(1)} %get-tuple-element.28), channel_id=1, source_target_pairs={{1,0},{2,1},{3,2},{0,3},{5,4},{6,5},{7,6},{4,7},{9,8},{10,9},{11,1... | collective-permute-start | bytes 632840 | tf_op jit(solution)/shard_map/ppermute | solution.py:271
  28.9 0.0 copy-done.7
  28.9 0.3 convolution_convert_fusion.lift_ref
  29.2 3.2 %collective-permute-done.1.before_ref = bf16[824,128]{1,0:T(8,128)(2,1)S(1)} collective-permute-done((bf16[824,128]{1,0:T(8,128)(2,1)S(1)}, bf16[824,128]{1,0:T(8,128)(2,1)S(1)}, u32[]{:S(2)}, u32[]{:S(2)}) %collective-permute-start.1) | collective-permute-done | bytes 210976 | tf_op jit(solution)/shard_map/ppermute | solution.py:270
  32.4 1.6 %collective-permute-done.2.after_ref = bf16[824,128]{1,0:T(8,128)(2,1)S(1)} collective-permute-done((bf16[824,128]{1,0:T(8,128)(2,1)S(1)}, bf16[824,128]{1,0:T(8,128)(2,1)S(1)}, u32[]{:S(2)}, u32[]{:S(2)}) %collective-permute-start.2) | collective-permute-done | bytes 210976 | tf_op jit(solution)/shard_map/ppermute | solution.py:271
  34.0 0.0 copy-done.5
  34.0 5.7 %stencil.1 = (f32[256,1024]{1,0:T(8,128)S(1)}, bf16[256,512]{1,0:T(8,128)(2,1)S(1)}, bf16[256,512]{1,0:T(8,128)(2,1)S(1)}) custom-call(bf16[824,1024]{1,0:T(8,128)(2,1)S(1)} %bitcast.55, f32[822,9]{1,0:T(8,128)S(1)} %copy.33.taps_ref, bf16[824,128]{1,0:T(8,128)(2,1)S(1)} %collective-permute-done.1.before_ref, ...), custom_call_target="tpu_custom_call" | custom-call | tf_op jit(solution)/shard_map/stencil/pallas_call | solution.py:273
  39.6 0.0 copy-start.3
  39.7 1.0 copy-done.3
  40.6 0.0 copy-start.17
  40.7 0.0 copy-start.18
  40.7 0.0 copy-start.19
  40.7 5.0 %all-to-all-done = bf16[64,96,128]{2,1,0:T(8,128)(2,1)} async-done(((bf16[64,96,128]{2,1,0:T(8,128)(2,1)}), bf16[64,96,128]{2,1,0:T(8,128)(2,1)}, u32[]{:S(2)}, u32[]{:S(2)}) %all-to-all-start) | async-done | bytes 1572896 | tf_op jit(solution)/shard_map/all_to_all | solution.py:219
  45.7 2.4 %reduce_sum.21 = bf16[8,96,128]{2,1,0:T(8,128)(2,1)} reduce(bf16[8,8,96,128]{3,2,1,0:T(8,128)(2,1)} %bitcast.5, bf16[]{:T(256)} %constant.28.clone.1), dimensions={0}, to_apply=%region_0.1 | reduce | flops 688128 | bytes 1769474 | tf_op jit(solution)/shard_map/reduce_sum | solution.py:291
  48.0 6.5 %all-to-all-start.1 = ((bf16[8,96,128]{2,1,0:T(8,128)(2,1)}), bf16[8,96,128]{2,1,0:T(8,128)(2,1)S(1)}, u32[]{:S(2)}, u32[]{:S(2)}) async-start(bf16[8,96,128]{2,1,0:T(8,128)(2,1)} %reduce_sum.21), calls=%async_computation.1 | async-start | bytes 393216 | tf_op jit(solution)/shard_map/all_to_all | solution.py:219
  54.5 0.0 copy-done.9
  54.5 0.2 fusion.29
  54.8 8.4 %all-to-all-done.1 = bf16[8,96,128]{2,1,0:T(8,128)(2,1)S(1)} async-done(((bf16[8,96,128]{2,1,0:T(8,128)(2,1)}), bf16[8,96,128]{2,1,0:T(8,128)(2,1)S(1)}, u32[]{:S(2)}, u32[]{:S(2)}) %all-to-all-start.1) | async-done | bytes 196640 | tf_op jit(solution)/shard_map/all_to_all | solution.py:219
  63.2 0.4 fusion.13
  63.6 0.0 copy-start.12
  63.7 11.0 %all_to_all.20 = bf16[8,96,128]{2,1,0:T(8,128)(2,1)S(1)} all-to-all(bf16[8,96,128]{2,1,0:T(8,128)(2,1)S(1)} %broadcast_in_dim.14), channel_id=1, replica_groups={{0,8,16,24,32,40,48,56},{64,72,80,88,96,104,112,120},{128,136,144,152,1..., dimensions={0} | all-to-all | bytes 393216 | tf_op jit(solution)/shard_map/all_to_all | solution.py:219
  74.7 1.4 %broadcast_in_dim.15 = bf16[8,8,96,128]{3,2,1,0:T(8,128)(2,1)} broadcast(bf16[8,96,128]{2,1,0:T(8,128)(2,1)S(1)} %all_to_all.20), dimensions={1,2,3} | broadcast | bytes 1769472 | tf_op jit(solution)/shard_map/broadcast_in_dim | solution.py:310
  76.1 0.0 copy-done.12
  76.1 4.3 %all-to-all-start.3 = ((bf16[64,96,128]{2,1,0:T(8,128)(2,1)}), bf16[64,96,128]{2,1,0:T(8,128)(2,1)}, u32[]{:S(2)}, u32[]{:S(2)}) async-start(bf16[64,96,128]{2,1,0:T(8,128)(2,1)} %bitcast.60), calls=%async_computation.3 | async-start | bytes 3145728 | tf_op jit(solution)/shard_map/all_to_all | solution.py:219
  80.4 0.0 copy-start.4
  80.4 0.0 copy-start.14
  80.4 6.5 %collective-permute-start.3 = (bf16[256,512]{1,0:T(8,128)(2,1)S(1)}, bf16[256,512]{1,0:T(8,128)(2,1)S(1)}, u32[]{:S(2)}, u32[]{:S(2)}) collective-permute-start(bf16[256,512]{1,0:T(8,128)(2,1)S(1)} %get-tuple-element.39), channel_id=1, source_target_pairs={{0,4},{4,8},{8,12},{12,16},{16,20},{20,24},{24,28},{28,32},{32,36}... | collective-permute-start | bytes 786440 | tf_op jit(solution)/shard_map/ppermute | solution.py:314
  87.0 1.9 %collective-permute-start.4 = (bf16[256,512]{1,0:T(8,128)(2,1)S(1)}, bf16[256,512]{1,0:T(8,128)(2,1)S(1)}, u32[]{:S(2)}, u32[]{:S(2)}) collective-permute-start(bf16[256,512]{1,0:T(8,128)(2,1)S(1)} %get-tuple-element.40), channel_id=1, source_target_pairs={{4,0},{8,4},{12,8},{16,12},{20,16},{24,20},{28,24},{32,28},{36,32}... | collective-permute-start | bytes 786440 | tf_op jit(solution)/shard_map/ppermute | solution.py:315
  88.9 0.8 fusion.4
  89.7 10.9 %collective-permute-done.3 = bf16[256,512]{1,0:T(8,128)(2,1)S(1)} collective-permute-done((bf16[256,512]{1,0:T(8,128)(2,1)S(1)}, bf16[256,512]{1,0:T(8,128)(2,1)S(1)}, u32[]{:S(2)}, u32[]{:S(2)}) %collective-permute-start.3) | collective-permute-done | bytes 262176 | tf_op jit(solution)/shard_map/ppermute | solution.py:314
  100.5 1.8 %collective-permute-done.4 = bf16[256,512]{1,0:T(8,128)(2,1)S(1)} collective-permute-done((bf16[256,512]{1,0:T(8,128)(2,1)S(1)}, bf16[256,512]{1,0:T(8,128)(2,1)S(1)}, u32[]{:S(2)}, u32[]{:S(2)}) %collective-permute-start.4) | collective-permute-done | bytes 262176 | tf_op jit(solution)/shard_map/ppermute | solution.py:315
  102.3 0.0 copy-done.4
  102.3 0.2 add_add_fusion.base_ref
  102.5 1.4 %all-to-all-done.3.dual_ref = bf16[64,96,128]{2,1,0:T(8,128)(2,1)} async-done(((bf16[64,96,128]{2,1,0:T(8,128)(2,1)}), bf16[64,96,128]{2,1,0:T(8,128)(2,1)}, u32[]{:S(2)}, u32[]{:S(2)}) %all-to-all-start.3) | async-done | bytes 1572896 | tf_op jit(solution)/shard_map/all_to_all | solution.py:219
  103.9 1.8 %gather.1 = (f32[96,1024]{1,0:T(8,128)S(1)}, bf16[96,1024]{1,0:T(8,128)(2,1)S(1)}) custom-call(s32[64]{0:T(128)S(1)} %get-tuple-element.25.slot_ref, bf16[64,96,128]{2,1,0:T(8,128)(2,1)} %all-to-all-done.3.dual_ref), custom_call_target="tpu_custom_call" | custom-call | tf_op jit(solution)/shard_map/gather/pallas_call | solution.py:319
  105.7 7.2 %collective-permute-start.5 = (bf16[96,1024]{1,0:T(8,128)(2,1)S(1)}, bf16[96,1024]{1,0:T(8,128)(2,1)S(1)}, u32[]{:S(2)}, u32[]{:S(2)}) collective-permute-start(bf16[96,1024]{1,0:T(8,128)(2,1)S(1)} %get-tuple-element.44), channel_id=1, source_target_pairs={{0,4},{4,0},{8,12},{12,8},{16,20},{20,16},{24,28},{28,24},{32,36},... | collective-permute-start | bytes 589832 | tf_op jit(solution)/shard_map/ppermute | solution.py:330
  113.0 1.0 collective-permute-done.5.other_ref
  114.0 2.5 %update.1 = bf16[822,2,512]{2,1,0:T(2,128)(2,1)} custom-call(f32[256,1024]{1,0:T(8,128)S(1)} %add_add_fusion.base_ref, f32[96,1024]{1,0:T(8,128)S(1)} %get-tuple-element.43.own_ref, bf16[96,1024]{1,0:T(8,128)(2,1)S(1)} %collective-permute-done.5.other_ref, bf16[256,96]{1,0:T(8,128)(2,1)S(1)} %convolution_convert_fusion.lift_ref, ...), custom_call_target="tpu_custom_call" | custom-call | tf_op jit(solution)/shard_map/update/pallas_call | solution.py:332
  (20 shorter events, 0.1 us)
Async XLA Ops:
  0.6 88.3 %copy-start = (bf16[256,822]{0,1:T(8,128)(2,1)S(1)}, bf16[256,822]{0,1:T(8,128)(2,1)}, u32[]{:S(2)}) copy-start(bf16[256,822]{0,1:T(8,128)(2,1)} %param.18) | copy-start | bytes 1262596
  0.6 1.5 %copy-start.1 = (bf16[822,2,512]{2,1,0:T(2,128)(2,1)S(1)}, bf16[822,2,512]{2,1,0:T(2,128)(2,1)}, u32[]{:S(2)}) copy-start(bf16[822,2,512]{2,1,0:T(2,128)(2,1)} %state_ref.1) | copy-start | bytes 5050372
  2.4 0.7 copy-start.13
  2.4 0.9 copy-start.8
  3.9 9.8 %collective-permute-start = (bf16[104,1024]{1,0:T(8,128)(2,1)S(1)}, bf16[104,1024]{1,0:T(8,128)(2,1)S(1)}, u32[]{:S(2)}, u32[]{:S(2)}) collective-permute-start(bf16[104,1024]{1,0:T(8,128)(2,1)S(1)} %fusion.15.own_ref), channel_id=1, source_target_pairs={{0,4},{4,0},{8,12},{12,8},{16,20},{20,16},{24,28},{28,24},{32,36},... | collective-permute-start | bytes 638984 | tf_op jit(solution)/shard_map/ppermute | solution.py:238
  13.7 8.1 %copy-start.10 = (f32[822,3,3]{0,2,1:T(4,128)S(1)}, f32[822,3,3]{0,2,1:T(4,128)}, u32[]{:S(2)}) copy-start(f32[822,3,3]{0,2,1:T(4,128)} %param.17) | copy-start | bytes 88780
  16.0 1.1 copy-start.2
  17.1 28.5 %all-to-all-start = ((bf16[64,96,128]{2,1,0:T(8,128)(2,1)}), bf16[64,96,128]{2,1,0:T(8,128)(2,1)}, u32[]{:S(2)}, u32[]{:S(2)}) async-start(bf16[64,96,128]{2,1,0:T(8,128)(2,1)} %copy-done.2), calls=%async_computation | async-start | bytes 3145728 | tf_op jit(solution)/shard_map/all_to_all | solution.py:219
  22.1 6.8 %copy-start.7 = (bf16[256,822]{0,1:T(8,128)(2,1)S(1)}, bf16[256,822]{0,1:T(8,128)(2,1)}, u32[]{:S(2)}) copy-start(bf16[256,822]{0,1:T(8,128)(2,1)} %param.20) | copy-start | bytes 1262596
  22.1 11.9 %copy-start.5 = (bf16[256,822]{0,1:T(8,128)(2,1)S(1)}, bf16[256,822]{0,1:T(8,128)(2,1)}, u32[]{:S(2)}) copy-start(bf16[256,822]{0,1:T(8,128)(2,1)} %param.19) | copy-start | bytes 1262596
  22.4 10.0 %collective-permute-start.1 = (bf16[824,128]{1,0:T(8,128)(2,1)S(1)}, bf16[824,128]{1,0:T(8,128)(2,1)S(1)}, u32[]{:S(2)}, u32[]{:S(2)}) collective-permute-start(bf16[824,128]{1,0:T(8,128)(2,1)S(1)} %get-tuple-element.27), channel_id=1, source_target_pairs={{0,1},{1,2},{2,3},{3,0},{4,5},{5,6},{6,7},{7,4},{8,9},{9,10},{10,1... | collective-permute-start | bytes 632840 | tf_op jit(solution)/shard_map/ppermute | solution.py:270
  25.5 8.5 %collective-permute-start.2 = (bf16[824,128]{1,0:T(8,128)(2,1)S(1)}, bf16[824,128]{1,0:T(8,128)(2,1)S(1)}, u32[]{:S(2)}, u32[]{:S(2)}) collective-permute-start(bf16[824,128]{1,0:T(8,128)(2,1)S(1)} %get-tuple-element.28), channel_id=1, source_target_pairs={{1,0},{2,1},{3,2},{0,3},{5,4},{6,5},{7,6},{4,7},{9,8},{10,9},{11,1... | collective-permute-start | bytes 632840 | tf_op jit(solution)/shard_map/ppermute | solution.py:271
  39.6 1.0 copy-start.3
  40.6 13.9 %copy-start.9 = (bf16[256,96]{0,1:T(8,128)(2,1)S(1)}, bf16[256,96]{0,1:T(8,128)(2,1)}, u32[]{:S(2)}) copy-start(bf16[256,96]{0,1:T(8,128)(2,1)} %param.28) | copy-start | bytes 147460
  40.6 13.9 %copy-start.11 = (bf16[96,1,128]{2,0,1:T(8,128)(2,1)S(1)}, bf16[96,1,128]{2,0,1:T(8,128)(2,1)}, u32[]{:S(2)}) copy-start(bf16[96,1,128]{2,0,1:T(8,128)(2,1)} %param.26) | copy-start | bytes 73732
  40.6 22.6 %copy-start.15 = (bf16[96,256]{1,0:T(8,128)(2,1)S(1)}, bf16[96,256]{1,0:T(8,128)(2,1)}, u32[]{:S(2)}) copy-start(bf16[96,256]{1,0:T(8,128)(2,1)} %param.30) | copy-start | bytes 147460
  40.6 22.6 %copy-start.16 = (bf16[256,96]{0,1:T(8,128)(2,1)S(1)}, bf16[256,96]{0,1:T(8,128)(2,1)}, u32[]{:S(2)}) copy-start(bf16[256,96]{0,1:T(8,128)(2,1)} %param.27) | copy-start | bytes 147460
  40.6 22.6 %copy-start.17 = (f32[96,1,128]{2,1,0:T(1,128)S(1)}, f32[96,1,128]{2,1,0:T(1,128)}, u32[]{:S(2)}) copy-start(f32[96,1,128]{2,1,0:T(1,128)} %param.24) | copy-start | bytes 147460
  40.7 22.6 %copy-start.18 = (s32[96,1,128]{2,1,0:T(1,128)S(1)}, s32[96,1,128]{2,1,0:T(1,128)}, u32[]{:S(2)}) copy-start(s32[96,1,128]{2,1,0:T(1,128)} %param.25) | copy-start | bytes 147460
  40.7 22.6 %copy-start.19 = (f32[256]{0:T(256)S(1)}, f32[256]{0:T(256)}, u32[]{:S(2)}) copy-start(f32[256]{0:T(256)} %param.29) | copy-start | bytes 3076
  48.0 15.2 %all-to-all-start.1 = ((bf16[8,96,128]{2,1,0:T(8,128)(2,1)}), bf16[8,96,128]{2,1,0:T(8,128)(2,1)S(1)}, u32[]{:S(2)}, u32[]{:S(2)}) async-start(bf16[8,96,128]{2,1,0:T(8,128)(2,1)} %reduce_sum.21), calls=%async_computation.1 | async-start | bytes 393216 | tf_op jit(solution)/shard_map/all_to_all | solution.py:219
  63.6 12.5 %copy-start.12 = (bf16[96,128]{1,0:T(8,128)(2,1)}, bf16[96,128]{1,0:T(8,128)(2,1)S(1)}, u32[]{:S(2)}) copy-start(bf16[96,128]{1,0:T(8,128)(2,1)S(1)} %fusion.13) | copy-start | bytes 73732
  76.1 27.8 %all-to-all-start.3 = ((bf16[64,96,128]{2,1,0:T(8,128)(2,1)}), bf16[64,96,128]{2,1,0:T(8,128)(2,1)}, u32[]{:S(2)}, u32[]{:S(2)}) async-start(bf16[64,96,128]{2,1,0:T(8,128)(2,1)} %bitcast.60), calls=%async_computation.3 | async-start | bytes 3145728 | tf_op jit(solution)/shard_map/all_to_all | solution.py:219
  80.4 21.9 %copy-start.4 = (f32[256,1024]{1,0:T(8,128)S(1)}, f32[256,1024]{1,0:T(8,128)}, u32[]{:S(2)}) copy-start(f32[256,1024]{1,0:T(8,128)} %copy-done.3) | copy-start | bytes 3145732
  80.4 21.9 %copy-start.14 = (f32[256]{0:T(256)S(1)}, f32[256]{0:T(256)}, u32[]{:S(2)}) copy-start(f32[256]{0:T(256)} %param.21) | copy-start | bytes 3076
  80.4 20.1 %collective-permute-start.3 = (bf16[256,512]{1,0:T(8,128)(2,1)S(1)}, bf16[256,512]{1,0:T(8,128)(2,1)S(1)}, u32[]{:S(2)}, u32[]{:S(2)}) collective-permute-start(bf16[256,512]{1,0:T(8,128)(2,1)S(1)} %get-tuple-element.39), channel_id=1, source_target_pairs={{0,4},{4,8},{8,12},{12,16},{16,20},{20,24},{24,28},{28,32},{32,36}... | collective-permute-start | bytes 786440 | tf_op jit(solution)/shard_map/ppermute | solution.py:314
  87.0 15.3 %collective-permute-start.4 = (bf16[256,512]{1,0:T(8,128)(2,1)S(1)}, bf16[256,512]{1,0:T(8,128)(2,1)S(1)}, u32[]{:S(2)}, u32[]{:S(2)}) collective-permute-start(bf16[256,512]{1,0:T(8,128)(2,1)S(1)} %get-tuple-element.40), channel_id=1, source_target_pairs={{4,0},{8,4},{12,8},{16,12},{20,16},{24,20},{28,24},{32,28},{36,32}... | collective-permute-start | bytes 786440 | tf_op jit(solution)/shard_map/ppermute | solution.py:315
  103.9 10.1 %copy-start.6 = (bf16[822,256]{1,0:T(8,128)(2,1)S(1)}, bf16[822,256]{1,0:T(8,128)(2,1)}, u32[]{:S(2)}) copy-start(bf16[822,256]{1,0:T(8,128)(2,1)} %wo_ref.1) | copy-start | bytes 1262596
  105.7 8.3 %collective-permute-start.5 = (bf16[96,1024]{1,0:T(8,128)(2,1)S(1)}, bf16[96,1024]{1,0:T(8,128)(2,1)S(1)}, u32[]{:S(2)}, u32[]{:S(2)}) collective-permute-start(bf16[96,1024]{1,0:T(8,128)(2,1)S(1)} %get-tuple-element.44), channel_id=1, source_target_pairs={{0,4},{4,0},{8,12},{12,8},{16,20},{20,16},{24,28},{28,24},{32,36},... | collective-permute-start | bytes 589832 | tf_op jit(solution)/shard_map/ppermute | solution.py:330
